TPU v7x, 128 devices: a whole 4x4x4 slice. The times are simulated.
128 devices in a mesh: gx: 16 (over z, x), gy: 8 (over y, core).
Axes of the slice: x: 4, y: 4, z: 4, core: 2. Of those that a mesh axis runs over, the one named last changes fastest.
Arguments:
- positions: float32 [3, 262144], P(None, ('gx', 'gy')), may hold values from -6 to 6
- velocities: float32 [3, 262144], P(None, ('gx', 'gy')), may hold values from -6 to 6
- masses: float32 [262144], P(('gx', 'gy')), may hold values from 0.25 to 4
- labels: int32 [262144, 1], P(('gx', 'gy')), may hold values from 0 to 1023; in each aligned block of 2048 rows (0 to 2047, 2048 to 4095, ...) at most 4 rows name the same one
- owner_slot: int32 [1024], replicated, may hold values from 0 to 1023, each once
- group_cap: int32 [1024], replicated, may hold values from 512 to 4095
Outputs:
- compact_index: int32 [262144], P(('gx', 'gy'))
- potential: float32 [262144], P(('gx', 'gy'))
- binding: float32 [262144], P(('gx', 'gy'))
- catalog: float32 [4, 1024], P(None, ('gx', 'gy'))
Inputs may be any that keep to these rules, and one draw needn't show every extreme that they name: `labels`: on each device's 2048 particles no label occurs more than 4 times; some label occurs exactly 4 times in some devices' particles; every label occurs somewhere. `owner_slot` is a permutation. Group g is owned by device owner_slot[g] // 8 (devices numbered along gx then gy) as its local group owner_slot[g] % 8.
All inputs are finite; a program needn't handle non-finite values.
Results may differ from a plain program's by a relative error of at most 0.0003.
Values sent between devices are 32-bit elements; how exact they have to be, the bound alone decides.
A program may use at most 64 MiB of HBM per device.

v0:
```python
import jax
import jax.numpy as jnp
from jax import lax
from jax.sharding import PartitionSpec as P

CAP = 2048


softening_sq = 0.0025


def potential_of(group_block, live_count):
    coords = group_block[0:3]
    weights = group_block[6]
    width = min(512, CAP)
    block_count = (live_count + width - 1) // width

    def row_step(row_block, result):
        row_start = row_block * width
        near = lax.dynamic_slice_in_dim(coords, row_start, width, 1)
        row_ids = row_start + jnp.arange(width, dtype=jnp.int32)

        def column_step(column_block, accum):
            column_start = column_block * width
            other = lax.dynamic_slice_in_dim(coords, column_start, width, 1)
            other_mass = lax.dynamic_slice_in_dim(weights, column_start, width, 0)
            column_ids = column_start + jnp.arange(width, dtype=jnp.int32)
            dist_sq = jnp.sum((near[:, :, None] - other[:, None, :]) ** 2, axis=0)
            inverse = jnp.where(
                row_ids[:, None] == column_ids[None, :], 0.0, lax.rsqrt(dist_sq + softening_sq)
            )
            return accum + jnp.sum(inverse * other_mass[None, :], axis=1)

        accum = lax.fori_loop(0, block_count, column_step, jnp.zeros((width,), jnp.float32))
        return lax.dynamic_update_slice_in_dim(result, -accum / CAP, row_start, 0)

    return lax.fori_loop(0, block_count, row_step, jnp.zeros((CAP,), jnp.float32))


def owner_work(received):
    items = received.shape[0]
    member_ranks = received[:, 7, :]
    valid = member_ranks >= 0.0
    target = jnp.where(valid, member_ranks.astype(jnp.int32), CAP)
    compact = (
        jnp.zeros((items, 7, CAP), jnp.float32)
        .at[jnp.arange(items)[:, None, None], jnp.arange(7)[None, :, None], target[:, None, :]]
        .set(received[:, 0:7, :], mode="drop")
    )
    live = jnp.sum(valid, axis=1, dtype=jnp.int32)
    pot = lax.map(lambda packed: potential_of(packed[0], packed[1]), (compact, live))
    weights = compact[:, 6, :]
    mass_sum = jnp.sum(weights, axis=1)
    bulk = jnp.sum(weights[:, None, :] * compact[:, 3:6, :], axis=2) / mass_sum[:, None]
    energy = 0.5 * jnp.sum((compact[:, 3:6, :] - bulk[:, :, None]) ** 2, axis=1) + pot
    both = jnp.stack([pot, energy], axis=1)
    safe = jnp.broadcast_to(jnp.minimum(target, CAP - 1)[:, None, :], (items, 2, target.shape[1]))
    answers = jnp.where(valid[:, None, :], jnp.take_along_axis(both, safe, axis=2), 0.0)
    stats = jnp.concatenate([mass_sum[:, None] / CAP, bulk], axis=1)
    return (answers, stats)


def shards(positions, velocities, masses, labels, owner_slot, group_cap):
    label_flat = labels[:, 0]
    count_dev = label_flat.shape[0]
    ngroups = owner_slot.shape[0]
    devices = lax.axis_size(("gx", "gy"))
    owned = ngroups // devices
    most_rows = 2 * count_dev // ngroups
    width_all = devices * most_rows
    row_width = min(512, count_dev)
    row_blocks = count_dev // row_width
    group_ids = jnp.arange(ngroups, dtype=jnp.int32)
    particle_ids = jnp.arange(count_dev, dtype=jnp.int32)
    block_starts = jnp.arange(row_blocks, dtype=jnp.int32) * row_width

    def tally(row_start):
        rows_label = lax.dynamic_slice_in_dim(label_flat, row_start, row_width, 0)
        rows_ids = row_start + jnp.arange(row_width, dtype=jnp.int32)
        same = (rows_label[:, None] == label_flat[None, :]) & (
            particle_ids[None, :] < rows_ids[:, None]
        )
        earlier = jnp.sum(same, axis=1, dtype=jnp.int32)
        hits = jnp.sum(rows_label[:, None] == group_ids[None, :], axis=0, dtype=jnp.int32)
        return (earlier, hits)

    earlier, hits = lax.map(tally, block_starts)
    local_rank = earlier.reshape(count_dev)
    counts = jnp.sum(hits, axis=0, dtype=jnp.int32)
    table = lax.all_gather(counts[None, :], ("gx", "gy"), axis=0, tiled=True)
    position = lax.axis_index(("gx", "gy"))
    below = (jnp.arange(devices, dtype=jnp.int32) < position)[:, None]
    prefix = jnp.sum(jnp.where(below, table, 0), axis=0, dtype=jnp.int32)
    totals = jnp.sum(table, axis=0, dtype=jnp.int32)
    limits = jnp.minimum(group_cap, CAP)
    kept_counts = jnp.minimum(totals, limits)
    starts = jnp.cumsum(kept_counts) - kept_counts
    lookup = jnp.stack([prefix, limits, starts, owner_slot], axis=1).astype(jnp.float32)

    def fetch(row_start):
        rows_label = lax.dynamic_slice_in_dim(label_flat, row_start, row_width, 0)
        onehot = (rows_label[:, None] == group_ids[None, :]).astype(jnp.float32)
        return jnp.dot(
            onehot, lookup, precision=lax.Precision.HIGHEST, preferred_element_type=jnp.float32
        )

    fetched = lax.map(fetch, block_starts).reshape(count_dev, 4).astype(jnp.int32)
    global_rank = fetched[:, 0] + local_rank
    keep = global_rank < fetched[:, 1]
    compact_index = jnp.where(keep, fetched[:, 2] + global_rank, -1)
    owner = fetched[:, 3] // owned
    local_group = fetched[:, 3] % owned
    dest = jnp.where(keep, owner * most_rows + local_rank, width_all)
    fields = jnp.concatenate(
        [positions, velocities, masses[None, :], global_rank.astype(jnp.float32)[None, :]], axis=0
    )
    outgoing = jnp.zeros((owned, 8, width_all), jnp.float32).at[:, 7, :].set(-1.0)
    outgoing = outgoing.at[local_group[:, None], jnp.arange(8)[None, :], dest[:, None]].set(
        jnp.transpose(fields), mode="drop"
    )
    answers, stats = owner_work(
        lax.all_to_all(outgoing, ("gx", "gy"), split_axis=2, concat_axis=2, tiled=True)
    )
    returned, stats = (
        lax.all_to_all(answers, ("gx", "gy"), split_axis=2, concat_axis=2, tiled=True),
        stats,
    )
    safe_dest = jnp.minimum(dest, width_all - 1)
    values = returned[local_group, :, safe_dest]
    potential = jnp.where(keep, values[:, 0], 0.0)
    binding = jnp.where(keep, values[:, 1], 0.0)
    catalog = jnp.transpose(stats)
    return (compact_index, potential, binding, catalog)


def solution(mesh):
    return jax.shard_map(
        shards,
        mesh=mesh,
        in_specs=(
            P(None, ("gx", "gy")),
            P(None, ("gx", "gy")),
            P(("gx", "gy")),
            P(("gx", "gy"), None),
            P(),
            P(),
        ),
        out_specs=(P(("gx", "gy")), P(("gx", "gy")), P(("gx", "gy")), P(None, ("gx", "gy"))),
        check_vma=False,
    )
```

profile of v0, /device:TPU:1, one launch (start us, length us, event | category | flops | bytes accessed | tf_op | source)
XLA Modules:
  0.0 398.8 jit_solution(8188834028946037595)
XLA Ops:
  0.7 24.2 %while.85 = (s32[]{:T(128)}, s32[4,512]{1,0:T(4,128)S(1)}, s32[4,1024]{1,0:T(4,128)S(1)}, s32[4]{0:T(128)S(1)}, s32[2048]{0:T(1024)}, /*index=5*/s32[2048,1]{0,1:T(1,128)}, s32[]{:T(128)}, s32[]{:T(128)}, s32[]{:T(128)}) while((s32[]{:T(128)}, s32[4,512]{1,0:T(4,128)S(1)}, s32[4,1024]{1,0:T(4,128)S(1)}, s32[4]{0:T(128)S(1)}, ...), condition=%wide.region_3.4_spmd.clone, body=%wide.region_0.3_spmd.clone.sunk | while | flops 6814725 | bytes 39067 | solution.py:87
  4.7 1.7 convert_reduce_fusion.5
  10.7 1.7 convert_reduce_fusion.5
  16.8 1.7 convert_reduce_fusion.5
  22.8 1.7 convert_reduce_fusion.5
  24.9 39.5 %all-gather = s32[131072]{0:T(1024)S(1)} all-gather(s32[1024]{0:T(1024)S(1)} %reduce_sum.99), channel_id=2, replica_groups=mesh['gx'=16,'gy'=8] {'gx','gy'}, dimensions={0}, use_global_device_ids=true | all-gather | bytes 528384 | tf_op jit(solution)/shard_map/all_gather | solution.py:90
  65.3 17.6 %while.86 = (s32[]{:T(128)}, f32[4,512,4]{1,2,0:T(4,128)S(1)}, s32[4]{0:T(128)S(1)}, s32[2048]{0:T(1024)}, f32[1024,4]{0,1:T(4,128)S(1)}, /*index=5*/s32[]{:T(128)}, s32[]{:T(128)}, s32[]{:T(128)}) while((s32[]{:T(128)}, f32[4,512,4]{1,2,0:T(4,128)S(1)}, s32[4]{0:T(128)S(1)}, s32[2048]{0:T(1024)}, f32[1024,4]{0,1:T(4,128)S(1)}, ...), condition=%wide.region_10.11_spmd.clone, body=%wide.region_9.10_spmd.clone.sunk | while | flops 25690116 | bytes 30859 | solution.py:107
  68.6 1.1 fusion.34
  73.0 1.1 fusion.34
  77.4 1.1 fusion.34
  81.8 1.1 fusion.34
  85.2 60.4 %scatter_fusion = f32[32768]{0:T(1024)S(1)} fusion(f32[32768]{0:T(1024)S(1)} %copy-done, s32[16384]{0:T(1024)S(1)} %reshape.207, f32[16384]{0:T(1024)S(1)} %reshape.209), kind=kCustom, calls=%fused_computation.2 | custom fusion | bytes 262144
  146.4 1.7 reshape.225
  148.1 5.2 %all-to-all-start = ((f32[128,1,256]{2,1,0:T(1,128)}), f32[128,1,256]{2,1,0:T(1,128)S(1)}, u32[]{:S(2)}, u32[]{:S(2)}) async-start(f32[128,1,256]{2,1,0:T(1,128)} %reshape.225), calls=%async_computation | async-start | bytes 262144 | tf_op jit(solution)/shard_map/all_to_all | solution.py:122
  153.4 10.0 %all-to-all-done = f32[128,1,256]{2,1,0:T(1,128)S(1)} async-done(((f32[128,1,256]{2,1,0:T(1,128)}), f32[128,1,256]{2,1,0:T(1,128)S(1)}, u32[]{:S(2)}, u32[]{:S(2)}) %all-to-all-start) | async-done | bytes 131104 | tf_op jit(solution)/shard_map/all_to_all | solution.py:122
  164.8 1.1 reshape.226
  166.0 2.0 slice.104
  167.9 2.2 copy.43
  171.5 105.3 %scatter_custom_fusion.1 = f32[114688]{0:T(1024)S(1)} fusion(s32[28672]{0:T(1024)S(1)} %reshape.213, f32[28672]{0:T(1024)S(1)} %reshape.215, f32[]{:T(128)} %constant.239.clone.1), kind=kCustom, calls=%fused_computation.35 | custom fusion | bytes 458756
  277.3 20.6 %while.84 = (s32[]{:T(128)}, f32[8,2048]{1,0:T(8,128)S(1)}, s32[8]{0:T(128)S(1)}, f32[8,7,2048]{2,0,1:T(8,128)S(1)}, s32[]{:T(128)}, /*index=5*/s32[]{:T(128)}, ...) while((s32[]{:T(128)}, f32[8,2048]{1,0:T(8,128)S(1)}, ...), condition=%wide.region_21.22_spmd, body=%wide.region_14.21_spmd.sunk | while | flops 3409951 | bytes 2302925 | solution.py:51
  278.7 1.0 while.87
  281.2 1.0 while.87
  283.8 1.0 while.87
  286.4 1.0 while.87
  289.0 1.0 while.87
  291.5 1.0 while.87
  294.1 1.0 while.87
  297.9 63.1 %gather_fusion.1 = f32[8192]{0:T(1024)S(1)} fusion(f32[8,2,2048]{2,0,1:T(8,128)S(1)} %pad_maximum_fusion, s32[8192]{0:T(1024)S(1)} %bitcast.99), kind=kCustom, calls=%fused_computation.1 | custom fusion | bytes 163840 | tf_op jit(solution)/shard_map/jit(take_along_axis)/gather | solution.py:58
  362.1 4.1 %all-to-all-start.1 = ((f32[8,2,512]{0,1,2:T(2,128)}), f32[8,2,512]{0,1,2:T(2,128)S(1)}, u32[]{:S(2)}, u32[]{:S(2)}) async-start(f32[8,2,512]{0,1,2:T(2,128)} %copy.40), calls=%async_computation.1 | async-start | bytes 1048576 | tf_op jit(solution)/shard_map/all_to_all | solution.py:125
  366.8 13.0 %all-to-all-done.1 = f32[8,2,512]{0,1,2:T(2,128)S(1)} async-done(((f32[8,2,512]{0,1,2:T(2,128)}), f32[8,2,512]{0,1,2:T(2,128)S(1)}, u32[]{:S(2)}, u32[]{:S(2)}) %all-to-all-start.1) | async-done | bytes 32800 | tf_op jit(solution)/shard_map/all_to_all | solution.py:125
  379.8 3.2 copy.41
  383.0 13.0 %gather_fusion = f32[2048,2]{1,0:T(8,128)S(1)} fusion(f32[8,2,512]{1,2,0:T(8,128)S(1)} %copy.41, s32[2048]{0:T(1024)S(1)} %bitcast.100), kind=kCustom, calls=%fused_computation | custom fusion | bytes 49152 | tf_op jit(solution)/shard_map/gather | solution.py:129
  (250 shorter events, 48.1 us)
Async XLA Ops:
  0.6 64.0 %copy-start.3 = (s32[1024]{0:T(1024)S(1)}, s32[1024]{0:T(1024)}, u32[]{:S(2)}) copy-start(s32[1024]{0:T(1024)} %param.23) | copy-start | bytes 12292
  0.6 64.6 %copy-start.5 = (s32[1024]{0:T(1024)S(1)}, s32[1024]{0:T(1024)}, u32[]{:S(2)}) copy-start(s32[1024]{0:T(1024)} %param.22) | copy-start | bytes 12292
  64.5 18.7 %copy-start.8 = (s32[3]{0:T(128)S(1)}, s32[3]{0:T(128)}, u32[]{:S(2)}) copy-start(s32[3]{0:T(128)} %constant.257) | copy-start | bytes 40
  64.5 18.7 %copy-start.7 = (s32[3]{0:T(128)S(1)}, s32[3]{0:T(128)}, u32[]{:S(2)}) copy-start(s32[3]{0:T(128)} %constant.260) | copy-start | bytes 40
  82.9 1.4 copy-start.1
  82.9 1.4 copy-start.2
  82.9 1.4 copy-start.4
  83.7 1.4 copy-start
  148.1 15.3 %all-to-all-start = ((f32[128,1,256]{2,1,0:T(1,128)}), f32[128,1,256]{2,1,0:T(1,128)S(1)}, u32[]{:S(2)}, u32[]{:S(2)}) async-start(f32[128,1,256]{2,1,0:T(1,128)} %reshape.225), calls=%async_computation | async-start | bytes 262144 | tf_op jit(solution)/shard_map/all_to_all | solution.py:122
  167.9 2.5 copy-start.9
  167.9 2.6 copy-start.6
  362.1 17.7 %all-to-all-start.1 = ((f32[8,2,512]{0,1,2:T(2,128)}), f32[8,2,512]{0,1,2:T(2,128)S(1)}, u32[]{:S(2)}, u32[]{:S(2)}) async-start(f32[8,2,512]{0,1,2:T(2,128)} %copy.40), calls=%async_computation.1 | async-start | bytes 1048576 | tf_op jit(solution)/shard_map/all_to_all | solution.py:125
where the time goes:
time: 400 us; the launch traced here: 399 us
  local copies, waits for them, and re-layouts  277 us (69%)
  blocking collectives  39.5 us (10%)
  waiting for transfers between devices  22.9 us (6%)
  loops' own time  22.3 us (6%)
  other arithmetic  22.1 us (6%)
  starting transfers between devices  9.36 us (2%)
  matrix products  4.35 us (1%)
    unnamed x33, local copies, waits for them, and re-layouts  172 us
    gather x2, local copies, waits for them, and re-layouts, owner_work(): jnp.take_along_axis(both, safe, axis=2)  63.1 us
    all_gather x1, blocking collectives, shards(): table = lax.all_gather(counts[None, :], ('gx', 'gy'), axis=0, tiled=True)  39.5 us
    gather x1, local copies, waits for them, and re-layouts, shards(): values = returned[local_group, :, safe_dest]  13 us
    all_to_all x1, waiting for transfers between devices, shards(): lax.all_to_all(answers, ('gx', 'gy'), split_axis=2, concat_axis=2, tiled=...  13 us
    all_to_all x1, waiting for transfers between devices, shards(): lax.all_to_all(outgoing, ('gx', 'gy'), split_axis=2, concat_axis=2, tiled...  9.98 us
  transfers between devices with their start and end apart: 2, of which 2 were waited for; matrix products, arithmetic and copies ran while one was open for 0% of the time, Pallas kernels for 0%

commit v1 on v0

v1 whole, which is shorter than its diff:
```python
import functools

import jax
import jax.numpy as jnp
from jax import lax
from jax.experimental import pallas as pl
from jax.experimental.pallas import tpu as pltpu
from jax.sharding import PartitionSpec as P

CAP = 2048
SOFTENING_SQ = 0.0025
MOST = 4
LANES = 128
MESH = pl.DeviceIdType.MESH
F32, BF16, I32 = jnp.float32, jnp.bfloat16, jnp.int32


def iota(shape, axis):
    return lax.broadcasted_iota(I32, shape, axis)


def onehot(index_row, depth):
    hit = iota((depth, index_row.shape[1]), 0) == index_row
    return jnp.where(hit, 1.0, 0.0).astype(BF16)


def parts_of(value, count):
    found = []
    for step in range(count):
        part = value.astype(BF16)
        found.append(part)
        if step < count - 1:
            value = value - part.astype(F32)
    return found


def dot(left, right):
    return lax.dot_general(left, right, (((1,), (0,)), ((), ())), preferred_element_type=F32)


def dot_nt(left, right):
    return lax.dot_general(left, right, (((1,), (1,)), ((), ())), preferred_element_type=F32)


def quad_sum(value):
    rows = value.shape[0]
    row = iota(value.shape, 0)
    for step in (1, 2):
        up = pltpu.roll(value, rows - step, 0)
        down = pltpu.roll(value, step, 0)
        value = value + jnp.where((row & step) == 0, up, down)
    return value


def exchange(here, out, mid, got, sends, recvs, local_sem, sizes):
    mx, my = here
    nx, ny = sizes
    own = pltpu.make_async_copy(
        out.at[:, pl.ds(my, 1), :], mid.at[:, pl.ds(my, 1), :], local_sem.at[0]
    )
    own.start()
    copies = []
    for step in range(1, ny):
        peer = lax.rem(my + step, ny)
        copy = pltpu.make_async_remote_copy(
            src_ref=out.at[:, pl.ds(peer, 1), :],
            dst_ref=mid.at[:, pl.ds(my, 1), :],
            send_sem=sends.at[step],
            recv_sem=recvs.at[step],
            device_id=(mx, peer),
            device_id_type=MESH,
        )
        copy.start()
        copies.append(copy)
    own.wait()
    for copy in copies:
        copy.wait()
    own = pltpu.make_async_copy(mid.at[mx], got.at[mx], local_sem.at[1])
    own.start()
    copies = []
    for step in range(1, nx):
        peer = lax.rem(mx + step, nx)
        copy = pltpu.make_async_remote_copy(
            src_ref=mid.at[peer],
            dst_ref=got.at[mx],
            send_sem=sends.at[ny + step],
            recv_sem=recvs.at[ny + step],
            device_id=(peer, my),
            device_id_type=MESH,
        )
        copy.start()
        copies.append(copy)
    own.wait()
    for copy in copies:
        copy.wait()


def kernel(
    sizes, lab_ref, lab16_ref, pos_ref, vel_ref, mass_ref, slot8_ref, slot_ref, cap_ref,
    index_ref, pot_ref, bind_ref, cat_ref,
    out1, mid1, got1, out2, mid2, got2, hot_label, hot_dest, hot_group, near, total,
    send1, recv1, send2, recv2, local_sem,
):
    nx, ny = sizes
    devices = nx * ny
    mx, my = lax.axis_index("gx"), lax.axis_index("gy")
    me = mx * ny + my
    count = lab_ref.shape[1]
    groups = slot_ref.shape[1]
    owned = groups // devices
    slots = owned * MOST
    blocks = count // LANES

    barrier = pltpu.get_barrier_semaphore()
    for step in range(1, ny):
        pl.semaphore_signal(barrier, inc=1, device_id=(mx, lax.rem(my + step, ny)), device_id_type=MESH)
    for step in range(1, nx):
        pl.semaphore_signal(barrier, inc=1, device_id=(lax.rem(mx + step, nx), my), device_id_type=MESH)

    label = lab_ref[...]
    label_high, label_low = label >> 7, label & 127
    hot_label[...] = onehot(label_low, LANES)
    slot8 = slot8_ref[...]
    table = jnp.concatenate([slot8 // owned, slot8 % owned], axis=0).astype(F32).astype(BF16)
    found = dot(table, hot_label[...])
    high_hit = iota((groups // LANES, count), 0) == label_high
    half = groups // LANES
    dest = jnp.sum(jnp.where(high_hit, found[:half], 0.0), axis=0, keepdims=True).astype(I32)
    local_group = jnp.sum(jnp.where(high_hit, found[half:], 0.0), axis=0, keepdims=True).astype(I32)

    columns = jnp.concatenate(
        [lab16_ref[...], jnp.zeros((LANES - blocks, LANES), I32)], axis=0
    ).astype(F32).T.astype(I32)
    ranks = []
    triangle = iota((LANES, LANES), 0) < iota((LANES, LANES), 1)
    for block in range(blocks):
        mine = label[:, block * LANES : (block + 1) * LANES]
        ranks.append(jnp.zeros((8, LANES), I32))
    for other in range(blocks):
        column = jnp.broadcast_to(columns[:, other : other + 1], (LANES, LANES))
        for block in range(other, blocks):
            mine = label[:, block * LANES : (block + 1) * LANES]
            same = column == mine
            if block == other:
                same = same & triangle
            hits = jnp.where(same, 1, 0)
            ranks[block] = ranks[block] + jnp.sum(hits.reshape(LANES // 8, 8, LANES), axis=0)
    rank = jnp.concatenate([jnp.sum(r, axis=0, keepdims=True) for r in ranks], axis=1)
    slot = local_group * MOST + rank

    hot_dest[...] = onehot(dest, devices)
    slot_hit = iota((slots, count), 0) == slot
    fields = [pos_ref[0:1, :], pos_ref[1:2, :], pos_ref[2:3, :], mass_ref[...],
              vel_ref[0:1, :], vel_ref[1:2, :], vel_ref[2:3, :]]
    split = [[part.astype(F32) for part in parts_of(field, 3)] for field in fields]
    for half_row in range(2):
        rows = None
        for part in range(3):
            chosen = [
                jnp.where(slot_hit, split[f][part], 0.0).astype(BF16)
                for f in range(half_row * 4, min(half_row * 4 + 4, 7))
            ]
            if half_row == 1:
                chosen.append(jnp.zeros((slots, count), BF16))
            product = dot_nt(hot_dest[...], jnp.concatenate(chosen, axis=0))
            rows = product if rows is None else rows + product
        out1[:, :, half_row * LANES : (half_row + 1) * LANES] = rows.reshape(nx, ny, LANES)

    slot_row = slot_ref[...]
    hot_group[...] = onehot(slot_row // owned, devices)
    row32 = iota((slots, 1), 0)
    limits = jnp.minimum(cap_ref[...], CAP).astype(F32)
    limit = jnp.sum(
        jnp.where(slot_row == me * owned + row32 // MOST, limits, 0.0), axis=1, keepdims=True
    )
    upper = jnp.where(iota((LANES, LANES), 0) < iota((LANES, LANES), 1), 1.0, 0.0).astype(BF16)

    pl.semaphore_wait(barrier, nx + ny - 2)
    exchange((mx, my), out1, mid1, got1, send1, recv1, local_sem.at[0], sizes)

    first = got1[:, :, :LANES].reshape(devices, LANES)
    second = got1[:, :, LANES:].reshape(devices, LANES)
    first_t, second_t = first.T, second.T
    mass_t = first_t[3 * slots :]
    valid = mass_t > 0.0
    tally = quad_sum(jnp.where(valid, 1.0, 0.0))
    before = dot(tally.astype(BF16), upper)
    member_rank = before + (row32 % MOST).astype(F32)
    keep = valid & (member_rank < limit)
    kept_mass = jnp.where(keep, mass_t, 0.0)
    kept_total = quad_sum(jnp.sum(jnp.where(keep, 1.0, 0.0), axis=1, keepdims=True))
    near[0 : LANES] = jnp.concatenate([first[:, : 3 * slots], jnp.concatenate(
        [kept_mass, jnp.zeros((LANES - slots, LANES), F32)], axis=0).T[:, :slots]], axis=1)
    near[LANES :] = first_t
    total[...] = jnp.zeros_like(total)
    offset = iota((8, LANES), 1) - iota((8, LANES), 0)

    def rows_of(step, carry):
        source = near[pl.ds(pl.multiple_of(step * 8, 8), 8), :]
        diagonal = offset == step * 8
        for group in range(owned):
            base = group * MOST
            here = [
                [jnp.broadcast_to(near[LANES + f * slots + base + r : LANES + f * slots + base + r + 1, :], (8, LANES)) for f in range(3)]
                for r in range(MOST)
            ]
            sums = [total[base + r] for r in range(MOST)]
            for other in range(MOST):
                there = [
                    jnp.broadcast_to(source[:, f * slots + base + other : f * slots + base + other + 1], (8, LANES))
                    for f in range(4)
                ]
                for r in range(MOST):
                    dx = here[r][0] - there[0]
                    dy = here[r][1] - there[1]
                    dz = here[r][2] - there[2]
                    inverse = lax.rsqrt(dx * dx + dy * dy + dz * dz + SOFTENING_SQ)
                    if r == other:
                        inverse = jnp.where(diagonal, 0.0, inverse)
                    sums[r] = sums[r] + inverse * there[3]
            for r in range(MOST):
                total[base + r] = sums[r]
        return carry

    lax.fori_loop(0, devices // 8, rows_of, 0)
    pot = jnp.sum(total[...], axis=1) * (-1.0 / CAP)

    mass_sum = quad_sum(jnp.sum(kept_mass, axis=1, keepdims=True))
    energy = None
    stats = [mass_sum * (1.0 / CAP)]
    for axis in range(3):
        speed = second_t[axis * slots : (axis + 1) * slots]
        bulk = quad_sum(jnp.sum(kept_mass * speed, axis=1, keepdims=True)) / mass_sum
        stats.append(bulk)
        apart = (speed - bulk) * (speed - bulk)
        energy = apart if energy is None else energy + apart
    energy = 0.5 * energy + pot
    pick = iota((slots, owned), 0) == iota((slots, owned), 1) * MOST
    for number, stat in enumerate(stats):
        cat_ref[number : number + 1, :] = jnp.sum(jnp.where(pick, stat, 0.0), axis=0, keepdims=True)
    reply = jnp.concatenate(
        [pot, energy, jnp.where(keep, member_rank, -1.0), jnp.broadcast_to(kept_total, (slots, LANES))],
        axis=0,
    )
    out2[...] = reply.T.reshape(nx, ny, LANES)
    exchange((mx, my), out2, mid2, got2, send2, recv2, local_sem.at[1], sizes)

    answer = got2[...].reshape(devices, LANES).T
    pieces = parts_of(answer, 3)
    kept_of = dot(pieces[0][3 * slots :], hot_group[...]) + dot(pieces[1][3 * slots :], hot_group[...])
    group_hit = iota((slots, groups), 0) == (slot_row % owned) * MOST
    kept_row = jnp.sum(jnp.where(group_hit, kept_of, 0.0), axis=0, keepdims=True)
    kept8 = jnp.concatenate(
        [kept_row[:, i * LANES : (i + 1) * LANES] for i in range(half)], axis=0
    )
    kept_parts = parts_of(kept8, 2)
    start8 = dot(kept_parts[0], upper) + dot(kept_parts[1], upper)
    row_total = jnp.sum(kept8, axis=1, keepdims=True)
    running = [jnp.zeros((1, 1), F32)]
    for i in range(half - 1):
        running.append(running[-1] + row_total[i : i + 1])
    start8 = start8 + jnp.concatenate(running, axis=0)
    start_parts = jnp.concatenate(parts_of(start8, 3), axis=0)
    start_found = dot(start_parts, hot_label[...])
    start_found = start_found[:half] + start_found[half : 2 * half] + start_found[2 * half :]
    start = jnp.sum(jnp.where(high_hit, start_found, 0.0), axis=0, keepdims=True)

    table = [piece[: 3 * slots] for piece in pieces]
    values = dot(table[0], hot_dest[...]) + dot(table[1], hot_dest[...]) + dot(table[2], hot_dest[...])
    chosen = [
        jnp.sum(jnp.where(slot_hit, values[v * slots : (v + 1) * slots], 0.0), axis=0, keepdims=True)
        for v in range(3)
    ]
    kept = chosen[2] >= 0.0
    index_ref[...] = jnp.where(kept, start + chosen[2], -1.0).astype(I32)
    pot_ref[...] = jnp.where(kept, chosen[0], 0.0)
    bind_ref[...] = jnp.where(kept, chosen[1], 0.0)


def shards(sizes, positions, velocities, masses, labels, owner_slot, group_cap):
    nx, ny = sizes
    count = masses.shape[0]
    groups = owner_slot.shape[0]
    owned = groups // (nx * ny)
    slots = owned * MOST
    vmem = pl.BlockSpec(memory_space=pltpu.VMEM)
    wide = lambda width: pltpu.VMEM((nx, ny, width), F32)
    index, pot, bind, catalog = pl.pallas_call(
        functools.partial(kernel, sizes),
        out_shape=(
            jax.ShapeDtypeStruct((1, count), I32),
            jax.ShapeDtypeStruct((1, count), F32),
            jax.ShapeDtypeStruct((1, count), F32),
            jax.ShapeDtypeStruct((4, owned), F32),
        ),
        in_specs=[vmem] * 8,
        out_specs=(vmem,) * 4,
        scratch_shapes=[
            wide(2 * LANES), wide(2 * LANES), wide(2 * LANES),
            wide(LANES), wide(LANES), wide(LANES),
            pltpu.VMEM((LANES, count), BF16),
            pltpu.VMEM((nx * ny, count), BF16),
            pltpu.VMEM((nx * ny, groups), BF16),
            pltpu.VMEM((2 * LANES, LANES), F32),
            pltpu.VMEM((slots, 8, LANES), F32),
            pltpu.SemaphoreType.DMA((nx + ny,)),
            pltpu.SemaphoreType.DMA((nx + ny,)),
            pltpu.SemaphoreType.DMA((nx + ny,)),
            pltpu.SemaphoreType.DMA((nx + ny,)),
            pltpu.SemaphoreType.DMA((2, 2)),
        ],
        compiler_params=pltpu.CompilerParams(collective_id=0, has_side_effects=True),
        name="unbind",
    )(
        labels.reshape(1, count), labels.reshape(count // LANES, LANES), positions, velocities,
        masses.reshape(1, count), owner_slot.reshape(groups // LANES, LANES),
        owner_slot.reshape(1, groups), group_cap.reshape(1, groups),
    )
    return (index.reshape(count), pot.reshape(count), bind.reshape(count), catalog)


def solution(mesh):
    sizes = (mesh.shape["gx"], mesh.shape["gy"])
    return jax.shard_map(
        functools.partial(shards, sizes),
        mesh=mesh,
        in_specs=(
            P(None, ("gx", "gy")),
            P(None, ("gx", "gy")),
            P(("gx", "gy")),
            P(("gx", "gy"), None),
            P(),
            P(),
        ),
        out_specs=(P(("gx", "gy")), P(("gx", "gy")), P(("gx", "gy")), P(None, ("gx", "gy"))),
        check_vma=False,
    )
```

time: 400 us -> 38.2 us (0.10)
  local copies, waits for them, and re-layouts: 277 us -> 3.34 us
  blocking collectives: 39.5 us -> 0 us
  Pallas kernels: 0 us -> 33.9 us
  waiting for transfers between devices: 22.9 us -> 0 us
  loops' own time: 22.3 us -> 0 us
  other arithmetic: 22.1 us -> 0 us
  starting transfers between devices: 9.36 us -> 0 us
  matrix products: 4.35 us -> 0 us
    unnamed x33 -> x12, local copies, waits for them, and re-layouts: 172 us -> 3.34 us
    gather x3 -> x0, local copies, waits for them, and re-layouts: 76.2 us -> none  [the longest x2 63.1 us: owner_work(): jnp.take_along_axis(both, safe, axis=2)]
    all_gather x1 -> x0, blocking collectives: 39.5 us -> none  [shards(): table = lax.all_gather(counts[None, :], ('gx', 'gy'), axis=0, tiled=True)]
    pallas_call x0 -> x1, Pallas kernels: none -> 33.9 us  [shards(): pl.pallas_call(functools.partial(kernel, sizes), out_shape=(jax.ShapeDtyp...]
    all_to_all x2 -> x0, waiting for transfers between devices: 22.9 us -> none  [the longest x1 13 us: shards(): lax.all_to_all(answers, ('gx', 'gy'), split_axis=2, concat_axis=2, tiled=...]
    another operation x19 -> x0, loops' own time: 22.3 us -> none  [the longest x1 7.94 us: shards(): earlier, hits = lax.map(tally, block_starts)]
    dynamic_slice x48 -> x0, local copies, waits for them, and re-layouts: 16.4 us -> none  [the longest x8 4.73 us: shards(): earlier, hits = lax.map(tally, block_starts)]
    reduce_sum x29 -> x0, other arithmetic: 13.7 us -> none  [the longest x4 6.66 us: tally(): earlier = jnp.sum(same, axis=1, dtype=jnp.int32)]
  transfers between devices with their start and end apart: 2 -> 0, of which waited for: 2 -> 0; matrix products, arithmetic and copies ran while one was open for 0% -> 0% of each run, Pallas kernels for 0% -> 0%
where the time goes in v1:
time: 38.2 us; the launch traced here: 37.9 us
  Pallas kernels  33.9 us (89%)
  local copies, waits for them, and re-layouts  3.34 us (9%)
  between operations  0.65 us (2%)
    pallas_call x1, Pallas kernels, shards(): pl.pallas_call(functools.partial(kernel, sizes), out_shape=(jax.ShapeDtyp...  33.9 us
    unnamed x12, local copies, waits for them, and re-layouts  3.34 us

profile of v1, /device:TPU:1, one launch (start us, length us, event | category | flops | bytes accessed | tf_op | source)
XLA Modules:
  0.0 37.9 jit_solution(198175909673715672)
XLA Ops:
  0.6 33.9 %unbind.1 = (s32[1,2048]{1,0:T(1,128)}, f32[1,2048]{1,0:T(1,128)}, f32[1,2048]{1,0:T(1,128)}, f32[4,8]{1,0:T(4,128)}) custom-call(s32[1,2048]{1,0:T(1,128)} %bitcast.9, s32[16,128]{1,0:T(8,128)} %bitcast.10, f32[3,2048]{1,0:T(4,128)} %pos_ref.1, f32[3,2048]{1,0:T(4,128)} %vel_ref.1, f32[1,2048]{1,0:T(1,128)} %bitcast.13, s32[8,128]{1,0:T(8,128)} %bitcast.11, ...), custom_call_target="tpu_custom_call" | custom-call | tf_op jit(solution)/shard_map/unbind/pallas_call | solution.py:288
  34.5 0.0 copy-start.2
  34.5 0.7 %copy-done.2 = s32[1,2048]{1,0:T(1,128)S(1)} copy-done((s32[1,2048]{1,0:T(1,128)S(1)}, s32[1,2048]{1,0:T(1,128)}, u32[]{:S(2)}) %copy-start.2) | copy-done | bytes 8216
  35.2 0.0 copy-start.1
  35.2 0.6 %copy.14 = s32[2048]{0:T(1024)} copy(s32[2048]{0:T(1024)S(1)} %bitcast.16) | data formatting | bytes 16384
  35.8 0.1 copy-done.1
  35.9 0.0 copy-start
  35.9 0.6 %copy.15 = f32[2048]{0:T(1024)} copy(f32[2048]{0:T(1024)S(1)} %bitcast.15) | data formatting | bytes 16384
  36.5 0.1 copy-done
  36.6 0.0 copy-start.3
  36.6 0.6 %copy.16 = f32[2048]{0:T(1024)} copy(f32[2048]{0:T(1024)S(1)} %bitcast.14) | data formatting | bytes 16384
  37.2 0.1 copy-done.3
  37.3 0.6 %copy.17 = f32[4,8]{1,0:T(4,128)} copy(f32[4,8]{1,0:T(4,128)S(1)} %copy-done.3) | data formatting | bytes 256
Async XLA Ops:
  34.5 0.7 %copy-start.2 = (s32[1,2048]{1,0:T(1,128)S(1)}, s32[1,2048]{1,0:T(1,128)}, u32[]{:S(2)}) copy-start(s32[1,2048]{1,0:T(1,128)} %get-tuple-element.8) | copy-start | bytes 24580
  35.2 0.7 %copy-start.1 = (f32[1,2048]{1,0:T(1,128)S(1)}, f32[1,2048]{1,0:T(1,128)}, u32[]{:S(2)}) copy-start(f32[1,2048]{1,0:T(1,128)} %get-tuple-element.9) | copy-start | bytes 24580
  35.9 0.7 %copy-start = (f32[1,2048]{1,0:T(1,128)S(1)}, f32[1,2048]{1,0:T(1,128)}, u32[]{:S(2)}) copy-start(f32[1,2048]{1,0:T(1,128)} %get-tuple-element.10) | copy-start | bytes 24580
  36.6 0.7 %copy-start.3 = (f32[4,8]{1,0:T(4,128)S(1)}, f32[4,8]{1,0:T(4,128)}, u32[]{:S(2)}) copy-start(f32[4,8]{1,0:T(4,128)} %get-tuple-element.19) | copy-start | bytes 388

commit v2 on v1

v2 whole, which is shorter than its diff:
```python
import functools

import jax
import jax.numpy as jnp
from jax import lax
from jax.experimental import pallas as pl
from jax.experimental.pallas import tpu as pltpu
from jax.sharding import PartitionSpec as P

CAP = 2048
SOFTENING_SQ = 0.0025
MOST = 4
LANES = 128
MESH = pl.DeviceIdType.MESH
F32, BF16, I32 = jnp.float32, jnp.bfloat16, jnp.int32


def iota(shape, axis):
    return lax.broadcasted_iota(I32, shape, axis)


def onehot(index_row, depth):
    hit = iota((depth, index_row.shape[1]), 0) == index_row
    return jnp.where(hit, 1.0, 0.0).astype(BF16)


def parts_of(value, count):
    found = []
    for step in range(count):
        part = value.astype(BF16)
        found.append(part)
        if step < count - 1:
            value = value - part.astype(F32)
    return found


def dot(left, right):
    return lax.dot_general(left, right, (((1,), (0,)), ((), ())), preferred_element_type=F32)


def dot_nt(left, right):
    return lax.dot_general(left, right, (((1,), (1,)), ((), ())), preferred_element_type=F32)


def quad_sum(value):
    lane = iota(value.shape, 1)
    for step in (1, 2):
        up = pltpu.roll(value, LANES - step, 1)
        down = pltpu.roll(value, step, 1)
        value = value + jnp.where((lane & step) == 0, up, down)
    return value


def far_first():
    ring = (0, 1, 2, 1)
    offsets = [(dz, dx, dy, dc) for dz in range(4) for dx in range(4) for dy in range(4) for dc in range(2)]
    offsets.sort(key=lambda o: (-(ring[o[0]] + ring[o[1]] + ring[o[2]]), -o[3]))
    return offsets[:-1]


def send_row(here, offset, out, got, send, recv, ny):
    mx, my = here
    dz, dx, dy, dc = offset
    px = ((mx // 4 + dz) % 4) * 4 + (mx + dx) % 4
    py = ((my // 2 + dy) % 4) * 2 + (my + dc) % 2
    pltpu.make_async_remote_copy(
        src_ref=out.at[pl.ds(px * ny + py, 1)],
        dst_ref=got.at[pl.ds(mx * ny + my, 1)],
        send_sem=send,
        recv_sem=recv,
        device_id=(px, py),
        device_id_type=MESH,
    ).start()


def kernel(
    sizes, lab_ref, lab16_ref, pos_ref, vel_ref, mass_ref, slot8_ref, slot_ref, cap_ref,
    reply_ref, place_ref, cat_ref,
    out1, spare1, got1, out2, spare2, got2, hot_dest, rows_ref, points, motion, member, halves,
    send1, recv1, send2, recv2, ready,
):
    nx, ny = sizes
    devices = nx * ny
    mx, my = lax.axis_index("gx"), lax.axis_index("gy")
    me = mx * ny + my
    count = lab_ref.shape[1]
    groups = slot_ref.shape[1]
    owned = groups // devices
    slots = owned * MOST
    blocks = count // LANES

    barrier = pltpu.get_barrier_semaphore()
    for step in range(1, ny):
        pl.semaphore_signal(barrier, inc=1, device_id=(mx, lax.rem(my + step, ny)), device_id_type=MESH)
    for step in range(1, nx):
        pl.semaphore_signal(barrier, inc=1, device_id=(lax.rem(mx + step, nx), my), device_id_type=MESH)

    label = lab_ref[...]
    label_high, label_low = label >> 7, label & 127
    slot8 = slot8_ref[...]
    table = jnp.concatenate([slot8 // owned, slot8 % owned], axis=0).astype(F32).astype(BF16)
    found = dot(table, onehot(label_low, LANES))
    high_hit = iota((groups // LANES, count), 0) == label_high
    half = groups // LANES
    dest = jnp.sum(jnp.where(high_hit, found[:half], 0.0), axis=0, keepdims=True).astype(I32)
    local_group = jnp.sum(jnp.where(high_hit, found[half:], 0.0), axis=0, keepdims=True).astype(I32)

    columns = jnp.concatenate(
        [lab16_ref[...], jnp.zeros((LANES - blocks, LANES), I32)], axis=0
    ).astype(F32).T.astype(I32)
    ranks = []
    triangle = iota((LANES, LANES), 0) < iota((LANES, LANES), 1)
    for block in range(blocks):
        mine = label[:, block * LANES : (block + 1) * LANES]
        ranks.append(jnp.zeros((8, LANES), I32))
    for other in range(blocks):
        column = jnp.broadcast_to(columns[:, other : other + 1], (LANES, LANES))
        for block in range(other, blocks):
            mine = label[:, block * LANES : (block + 1) * LANES]
            same = column == mine
            if block == other:
                same = same & triangle
            hits = jnp.where(same, 1, 0)
            ranks[block] = ranks[block] + jnp.sum(hits.reshape(LANES // 8, 8, LANES), axis=0)
    rank = jnp.concatenate([jnp.sum(r, axis=0, keepdims=True) for r in ranks], axis=1)
    slot = local_group * MOST + rank
    place_ref[...] = dest * slots + slot

    hot_dest[...] = onehot(dest, devices)
    slot_hit = iota((slots, count), 0) == slot
    fields = [mass_ref[...], pos_ref[0:1, :], pos_ref[1:2, :], pos_ref[2:3, :],
              vel_ref[0:1, :], vel_ref[1:2, :], vel_ref[2:3, :]]
    split = [[part.astype(F32) for part in parts_of(field, 3)] for field in fields]
    for half_row in range(2):
        rows = None
        for part in range(3):
            chosen = [
                jnp.where(slot_hit, split[f][part], 0.0).astype(BF16)
                for f in range(half_row * 4, min(half_row * 4 + 4, 7))
            ]
            if half_row == 1:
                chosen.append(jnp.zeros((slots, count), BF16))
            product = dot_nt(hot_dest[...], jnp.concatenate(chosen, axis=0))
            rows = product if rows is None else rows + product
        out1[:, half_row * LANES : (half_row + 1) * LANES] = rows

    slot_row = slot_ref[...]
    mine = jnp.where(iota((LANES, groups), 0) // MOST == slot_row - me * owned, 1.0, 0.0).astype(BF16)
    limits = jnp.minimum(cap_ref[...], CAP)
    limit_parts = jnp.concatenate([limits // 64, limits % 64], axis=0).astype(F32).astype(BF16)
    limit = dot_nt(limit_parts, mine)
    limit = limit[0:1] * 64.0 + limit[1:2]
    lower = jnp.where(iota((LANES, LANES), 1) < iota((LANES, LANES), 0), 1.0, 0.0).astype(BF16)
    quarter = (iota((1, LANES), 1) % MOST).astype(F32)

    pl.semaphore_wait(barrier, nx + ny - 2)
    for step in range(1, nx):
        pl.semaphore_signal(ready, inc=1, device_id=(lax.rem(mx + step, nx), my), device_id_type=MESH)
    pl.semaphore_wait(ready, nx - 1)
    here = (mx, my)
    for offset in far_first():
        send_row(here, offset, out1, got1, send1, recv1, ny)
    own = pl.ds(me, 1)
    pltpu.make_async_copy(out1.at[own], got1.at[own], recv1).start()
    pltpu.make_async_copy(out1.at[own], spare1.at[own], send1).start()
    pltpu.make_async_copy(out1, out1, send1).wait()
    pltpu.make_async_copy(got1, got1, recv1).wait()

    first = got1[:, :LANES]
    lane = iota((1, LANES), 1)
    is_mass = lane < slots
    valid = is_mass & (first > 0.0)
    tally = quad_sum(jnp.where(valid, 1.0, 0.0))
    member_rank = dot(lower, tally.astype(BF16)) + quarter
    keep = valid & (member_rank < limit)
    points[...] = jnp.where(is_mass & ~keep, 0.0, first)
    rows_ref[...] = points[...].T
    kept_mass = jnp.where(keep, first, 0.0)
    kept_total = quad_sum(jnp.sum(jnp.where(keep, 1.0, 0.0), axis=0, keepdims=True))
    mass_sum = quad_sum(jnp.sum(kept_mass, axis=0, keepdims=True))
    second = got1[:, LANES:]
    stats = [mass_sum * (1.0 / CAP)]
    energy = None
    for axis in range(3):
        speed = second if axis == 0 else pltpu.roll(second, LANES - axis * slots, 1)
        bulk = quad_sum(jnp.sum(kept_mass * speed, axis=0, keepdims=True)) / mass_sum
        stats.append(bulk)
        apart = (speed - bulk) * (speed - bulk)
        energy = apart if energy is None else energy + apart
    motion[...] = jnp.where((lane >= slots) & (lane < 2 * slots), pltpu.roll(0.5 * energy, slots, 1), 0.0)
    pick = iota((LANES, owned), 0) == iota((LANES, owned), 1) * MOST
    stat_rows = jnp.concatenate(stats + [jnp.zeros((LANES - 4, LANES), F32)], axis=0).T
    for number in range(4):
        cat_ref[number : number + 1, :] = jnp.sum(
            jnp.where(pick, stat_rows[:, number : number + 1], 0.0), axis=0, keepdims=True
        )
    rank_or_not = jnp.where(keep, member_rank, -1.0)
    member[...] = jnp.where(
        lane < 3 * slots,
        pltpu.roll(rank_or_not, 2 * slots, 1),
        pltpu.roll(jnp.broadcast_to(kept_total, (devices, LANES)), 3 * slots, 1),
    )
    offset8 = iota((8, LANES), 1) - iota((8, LANES), 0)
    lane8 = iota((8, LANES), 1)
    spot8 = lane8 % slots
    ones = jnp.ones((2 * LANES, LANES), BF16)

    def order(digit):
        half, odd = digit // 2, digit % 2
        return (1 - half) * (2 - odd) + half * (3 - 3 * odd)

    def column_of(step):
        dz, dx = order(step // 4), order(step % 4)
        return ((mx // 4 + dz) % 4) * 4 + (mx + dx) % 4

    def conclude(px):
        at = pl.ds(pl.multiple_of(px * 8, 8), 8)
        sums = dot(halves[...], ones)
        pot = jnp.zeros((8, LANES), F32)
        for spot in range(slots):
            pot = jnp.where(spot8 == spot, sums[spot * 8 : spot * 8 + 8], pot)
        both = pot * (-1.0 / CAP) + motion[at, :]
        out2[at, :] = jnp.where(lane8 < 2 * slots, both, member[at, :])

    def send_block(px):
        for peer in range(ny):

            @pl.when((px - mx) * (px - mx) + (peer - my) * (peer - my) > 0)
            def _():
                pltpu.make_async_remote_copy(
                    src_ref=out2.at[pl.ds(px * ny + peer, 1)],
                    dst_ref=got2.at[own],
                    send_sem=send2,
                    recv_sem=recv2,
                    device_id=(px, peer),
                    device_id_type=MESH,
                ).start()

    def block_of(step, carry):
        px = column_of(step)
        before = column_of((step + nx - 1) % nx)
        conclude(before)
        target = points[pl.ds(pl.multiple_of(px * 8, 8), 8), :]
        diagonal = offset8 == px * 8
        for group in range(owned):
            base = group * MOST
            there = [
                [jnp.broadcast_to(rows_ref[f * slots + base + r : f * slots + base + r + 1, :], (8, LANES)) for f in range(4)]
                for r in range(MOST)
            ]
            totals = []
            for r in range(MOST):
                spot = base + r
                px_, py_, pz_ = [
                    jnp.broadcast_to(target[:, f * slots + spot : f * slots + spot + 1], (8, LANES))
                    for f in range(1, 4)
                ]
                total = None
                for other in range(MOST):
                    ax = px_ - there[other][1]
                    ay = py_ - there[other][2]
                    az = pz_ - there[other][3]
                    inverse = lax.rsqrt(ax * ax + ay * ay + az * az + SOFTENING_SQ)
                    if r == other:
                        inverse = jnp.where(diagonal, 0.0, inverse)
                    term = inverse * there[other][0]
                    total = term if total is None else total + term
                totals.append(total)
            for pair in range(0, MOST, 2):
                two = jnp.concatenate(totals[pair : pair + 2], axis=0)
                high, low = parts_of(two, 2)
                lines = pl.ds((base + pair) * 8, 16)
                halves[lines, :LANES] = high
                halves[lines, LANES:] = low

        @pl.when(step > 0)
        def _():
            send_block(before)

        return carry

    halves[...] = jnp.zeros_like(halves)
    lax.fori_loop(0, nx, block_of, 0)
    conclude(mx)
    send_block(mx)
    pltpu.make_async_copy(out2.at[own], got2.at[own], recv2).start()
    pltpu.make_async_copy(out2.at[own], spare2.at[own], send2).start()
    pltpu.make_async_copy(out2, out2, send2).wait()
    pltpu.make_async_copy(got2, got2, recv2).wait()
    reply_ref[...] = got2[...]


def finish(lab_ref, slot_ref, place_ref, reply_ref, cat_in, index_ref, pot_ref, bind_ref, cat_ref):
    count = lab_ref.shape[1]
    groups = slot_ref.shape[1]
    devices = reply_ref.shape[0]
    half = groups // LANES
    owned = groups // devices
    slots = owned * MOST
    cat_ref[...] = cat_in[...]
    label = lab_ref[...]
    label_high, label_low = label >> 7, label & 127
    high_hit = iota((half, count), 0) == label_high
    place = place_ref[...]
    hot_dest = onehot(place // slots, devices)
    slot_hit = iota((slots, count), 0) == place % slots
    slot_row = slot_ref[...]
    hot_group = onehot(slot_row // owned, devices)
    upper = jnp.where(iota((LANES, LANES), 0) < iota((LANES, LANES), 1), 1.0, 0.0).astype(BF16)

    answer = reply_ref[...].T
    pieces = parts_of(answer, 3)
    kept_of = dot(pieces[0][3 * slots :], hot_group) + dot(pieces[1][3 * slots :], hot_group)
    group_hit = iota((slots, groups), 0) == (slot_row % owned) * MOST
    kept_row = jnp.sum(jnp.where(group_hit, kept_of, 0.0), axis=0, keepdims=True)
    kept8 = jnp.concatenate(
        [kept_row[:, i * LANES : (i + 1) * LANES] for i in range(half)], axis=0
    )
    kept_parts = parts_of(kept8, 2)
    start8 = dot(kept_parts[0], upper) + dot(kept_parts[1], upper)
    row_total = jnp.sum(kept8, axis=1, keepdims=True)
    running = [jnp.zeros((1, 1), F32)]
    for i in range(half - 1):
        running.append(running[-1] + row_total[i : i + 1])
    start8 = start8 + jnp.concatenate(running, axis=0)
    start_parts = jnp.concatenate(parts_of(start8, 3), axis=0)
    start_found = dot(start_parts, onehot(label_low, LANES))
    start_found = start_found[:half] + start_found[half : 2 * half] + start_found[2 * half :]
    start = jnp.sum(jnp.where(high_hit, start_found, 0.0), axis=0, keepdims=True)

    table = [piece[: 3 * slots] for piece in pieces]
    values = dot(table[0], hot_dest) + dot(table[1], hot_dest) + dot(table[2], hot_dest)
    chosen = [
        jnp.sum(jnp.where(slot_hit, values[v * slots : (v + 1) * slots], 0.0), axis=0, keepdims=True)
        for v in range(3)
    ]
    kept = chosen[2] >= 0.0
    index_ref[...] = jnp.where(kept, start + chosen[2], -1.0).astype(I32)
    pot_ref[...] = jnp.where(kept, chosen[0], 0.0)
    bind_ref[...] = jnp.where(kept, chosen[1], 0.0)


def shards(sizes, positions, velocities, masses, labels, owner_slot, group_cap):
    nx, ny = sizes
    count = masses.shape[0]
    groups = owner_slot.shape[0]
    owned = groups // (nx * ny)
    slots = owned * MOST
    vmem = pl.BlockSpec(memory_space=pltpu.VMEM)
    devices = nx * ny
    wide = lambda width: pltpu.VMEM((devices, width), F32)
    label_row = labels.reshape(1, count)
    slot_row = owner_slot.reshape(1, groups)
    reply, place, catalog = pl.pallas_call(
        functools.partial(kernel, sizes),
        out_shape=(
            jax.ShapeDtypeStruct((devices, LANES), F32),
            jax.ShapeDtypeStruct((1, count), I32),
            jax.ShapeDtypeStruct((4, owned), F32),
        ),
        in_specs=[vmem] * 8,
        out_specs=(vmem,) * 3,
        scratch_shapes=[
            *[wide(2 * LANES)] * 3,
            *[wide(LANES)] * 3,
            pltpu.VMEM((devices, count), BF16),
            *[wide(LANES)] * 4,
            pltpu.VMEM((slots * 8, 2 * LANES), BF16),
            *[pltpu.SemaphoreType.DMA] * 4,
            pltpu.SemaphoreType.REGULAR,
        ],
        compiler_params=pltpu.CompilerParams(collective_id=0, has_side_effects=True),
        name="unbind",
    )(
        label_row, labels.reshape(count // LANES, LANES), positions, velocities,
        masses.reshape(1, count), owner_slot.reshape(groups // LANES, LANES),
        slot_row, group_cap.reshape(1, groups),
    )
    row = lambda dtype: jax.ShapeDtypeStruct((1, count), dtype)
    index, pot, bind, catalog = pl.pallas_call(
        finish,
        out_shape=(row(I32), row(F32), row(F32), jax.ShapeDtypeStruct((4, owned), F32)),
        in_specs=[vmem] * 5,
        out_specs=(vmem,) * 4,
        name="finish",
    )(label_row, slot_row, place, reply, catalog)
    return (index.reshape(count), pot.reshape(count), bind.reshape(count), catalog)


def solution(mesh):
    sizes = (mesh.shape["gx"], mesh.shape["gy"])
    return jax.shard_map(
        functools.partial(shards, sizes),
        mesh=mesh,
        in_specs=(
            P(None, ("gx", "gy")),
            P(None, ("gx", "gy")),
            P(("gx", "gy")),
            P(("gx", "gy"), None),
            P(),
            P(),
        ),
        out_specs=(P(("gx", "gy")), P(("gx", "gy")), P(("gx", "gy")), P(None, ("gx", "gy"))),
        check_vma=False,
    )
```

time: 38.2 us -> 33 us (0.86)
  local copies, waits for them, and re-layouts: 3.34 us -> 0 us
  Pallas kernels: 33.9 us -> 32.2 us
    pallas_call x1, Pallas kernels: 33.9 us -> 29.6 us  [shards(): pl.pallas_call(functools.partial(kernel, sizes), out_shape=(jax.ShapeDtyp...]
    unnamed x12 -> x0, local copies, waits for them, and re-layouts: 3.34 us -> none
    pallas_call x0 -> x1, Pallas kernels: none -> 2.56 us  [shards(): pl.pallas_call(finish, out_shape=(row(I32), row(F32), row(F32), jax.Shape...]
where the time goes in v2:
time: 33 us; the launch traced here: 32.8 us
  Pallas kernels  32.2 us (98%)
  between operations  0.64 us (2%)
    pallas_call x1, Pallas kernels, shards(): pl.pallas_call(functools.partial(kernel, sizes), out_shape=(jax.ShapeDtyp...  29.6 us
    pallas_call x1, Pallas kernels, shards(): pl.pallas_call(finish, out_shape=(row(I32), row(F32), row(F32), jax.Shape...  2.56 us

profile of v2, /device:TPU:1, one launch (start us, length us, event | category | flops | bytes accessed | tf_op | source)
XLA Modules:
  0.0 32.8 jit_solution(7540074940700202621)
XLA Ops:
  0.6 29.6 %unbind.1 = (f32[128,128]{1,0:T(8,128)}, s32[1,2048]{1,0:T(1,128)}, f32[4,8]{1,0:T(4,128)}) custom-call(s32[1,2048]{1,0:T(1,128)} %bitcast.9, s32[16,128]{1,0:T(8,128)} %bitcast.10, f32[3,2048]{1,0:T(4,128)} %pos_ref.1, f32[3,2048]{1,0:T(4,128)} %vel_ref.1, f32[1,2048]{1,0:T(1,128)} %bitcast.15, s32[8,128]{1,0:T(8,128)} %bitcast.13, s32[1,1024]{1,0:T(1,128)} %bitcast.12, ...), custom_call_target="tpu_custom_call" | custom-call | tf_op jit(solution)/shard_map/unbind/pallas_call | solution.py:354
  30.3 2.6 %finish.1 = (s32[1,2048]{1,0:T(1,128)}, f32[1,2048]{1,0:T(1,128)}, f32[1,2048]{1,0:T(1,128)}, f32[4,8]{1,0:T(4,128)}) custom-call(s32[1,2048]{1,0:T(1,128)} %bitcast.11, s32[1,1024]{1,0:T(1,128)} %bitcast.14, s32[1,2048]{1,0:T(1,128)} %get-tuple-element.11.place_ref, f32[128,128]{1,0:T(8,128)} %get-tuple-element.12.reply_ref, f32[4,8]{1,0:T(4,128)} %get-tuple-element.13.cat_in), custom_call_target="tpu_custom_call" | custom-call | tf_op jit(solution)/shard_map/finish/pallas_call | solution.py:380

commit v3 on v2

--- a/solution.py
+++ b/solution.py
@@ -32,6 +32,17 @@
         if step < count - 1:
             value = value - part.astype(F32)
     return found
+
+
+def pick_lanes(table, index_row):
+    found = []
+    for at in range(0, index_row.shape[1], LANES):
+        index = jnp.broadcast_to(index_row[:, at : at + LANES], (8, LANES))
+        found.append(jnp.concatenate([
+            jnp.take_along_axis(table[row : row + 8], index, axis=1)
+            for row in range(0, table.shape[0], 8)
+        ], axis=0))
+    return jnp.concatenate(found, axis=1)
 
 
 def dot(left, right):
@@ -74,10 +85,12 @@
 
 
 def kernel(
-    sizes, lab_ref, lab16_ref, pos_ref, vel_ref, mass_ref, slot8_ref, slot_ref, cap_ref,
-    reply_ref, place_ref, cat_ref,
-    out1, spare1, got1, out2, spare2, got2, hot_dest, rows_ref, points, motion, member, halves,
-    send1, recv1, send2, recv2, ready,
+    sizes, lab_hbm, lab16_hbm, pos_hbm, vel_hbm, mass_hbm, slot8_hbm, slot_hbm, cap_hbm,
+    index_ref, pot_ref, bind_ref, cat_ref,
+    lab_ref, lab16_ref, pos_ref, vel_ref, mass_ref, slot8_ref, slot_ref, cap_ref,
+    out1, spare1, got1, out2, spare2, got2, hot_dest,
+    rows_ref, points, motion, member, halves,
+    load_sems, send1, recv1, send2, recv2, ready,
 ):
     nx, ny = sizes
     devices = nx * ny
@@ -88,22 +101,34 @@
     owned = groups // devices
     slots = owned * MOST
     blocks = count // LANES
-
+    half = groups // LANES
+
+    loads = [
+        pltpu.make_async_copy(source, place, load_sems.at[number])
+        for number, (source, place) in enumerate((
+            (lab_hbm, lab_ref), (slot8_hbm, slot8_ref), (lab16_hbm, lab16_ref), (mass_hbm, mass_ref),
+            (pos_hbm, pos_ref), (vel_hbm, vel_ref), (slot_hbm, slot_ref), (cap_hbm, cap_ref),
+        ))
+    ]
+    for load in loads:
+        load.start()
     barrier = pltpu.get_barrier_semaphore()
+    for step in range(1, nx):
+        pl.semaphore_signal(barrier, inc=1, device_id=(lax.rem(mx + step, nx), my), device_id_type=MESH)
     for step in range(1, ny):
         pl.semaphore_signal(barrier, inc=1, device_id=(mx, lax.rem(my + step, ny)), device_id_type=MESH)
-    for step in range(1, nx):
-        pl.semaphore_signal(barrier, inc=1, device_id=(lax.rem(mx + step, nx), my), device_id_type=MESH)
+    for load in loads:
+        load.wait()
 
     label = lab_ref[...]
     label_high, label_low = label >> 7, label & 127
     slot8 = slot8_ref[...]
     table = jnp.concatenate([slot8 // owned, slot8 % owned], axis=0).astype(F32).astype(BF16)
-    found = dot(table, onehot(label_low, LANES))
-    high_hit = iota((groups // LANES, count), 0) == label_high
-    half = groups // LANES
-    dest = jnp.sum(jnp.where(high_hit, found[:half], 0.0), axis=0, keepdims=True).astype(I32)
-    local_group = jnp.sum(jnp.where(high_hit, found[half:], 0.0), axis=0, keepdims=True).astype(I32)
+    high_hit = iota((half, count), 0) == label_high
+    owner = jnp.sum(
+        jnp.where(high_hit, pick_lanes(slot8_ref[...], label_low), 0), axis=0, keepdims=True
+    )
+    dest, local_group = owner // owned, owner % owned
 
     columns = jnp.concatenate(
         [lab16_ref[...], jnp.zeros((LANES - blocks, LANES), I32)], axis=0
@@ -124,7 +149,6 @@
             ranks[block] = ranks[block] + jnp.sum(hits.reshape(LANES // 8, 8, LANES), axis=0)
     rank = jnp.concatenate([jnp.sum(r, axis=0, keepdims=True) for r in ranks], axis=1)
     slot = local_group * MOST + rank
-    place_ref[...] = dest * slots + slot
 
     hot_dest[...] = onehot(dest, devices)
     slot_hit = iota((slots, count), 0) == slot
@@ -154,9 +178,9 @@
     quarter = (iota((1, LANES), 1) % MOST).astype(F32)
 
     pl.semaphore_wait(barrier, nx + ny - 2)
-    for step in range(1, nx):
-        pl.semaphore_signal(ready, inc=1, device_id=(lax.rem(mx + step, nx), my), device_id_type=MESH)
-    pl.semaphore_wait(ready, nx - 1)
+    for step in range(1, ny):
+        pl.semaphore_signal(ready, inc=1, device_id=(mx, lax.rem(my + step, ny)), device_id_type=MESH)
+    pl.semaphore_wait(ready, ny - 1)
     here = (mx, my)
     for offset in far_first():
         send_row(here, offset, out1, got1, send1, recv1, ny)
@@ -188,17 +212,16 @@
         apart = (speed - bulk) * (speed - bulk)
         energy = apart if energy is None else energy + apart
     motion[...] = jnp.where((lane >= slots) & (lane < 2 * slots), pltpu.roll(0.5 * energy, slots, 1), 0.0)
-    pick = iota((LANES, owned), 0) == iota((LANES, owned), 1) * MOST
-    stat_rows = jnp.concatenate(stats + [jnp.zeros((LANES - 4, LANES), F32)], axis=0).T
-    for number in range(4):
-        cat_ref[number : number + 1, :] = jnp.sum(
-            jnp.where(pick, stat_rows[:, number : number + 1], 0.0), axis=0, keepdims=True
-        )
     rank_or_not = jnp.where(keep, member_rank, -1.0)
     member[...] = jnp.where(
         lane < 3 * slots,
         pltpu.roll(rank_or_not, 2 * slots, 1),
-        pltpu.roll(jnp.broadcast_to(kept_total, (devices, LANES)), 3 * slots, 1),
+        jnp.broadcast_to(
+            jnp.take_along_axis(
+                jnp.broadcast_to(kept_total, (8, LANES)), (iota((8, LANES), 1) % owned) * MOST, axis=1
+            )[0:1],
+            (devices, LANES),
+        ),
     )
     offset8 = iota((8, LANES), 1) - iota((8, LANES), 0)
     lane8 = iota((8, LANES), 1)
@@ -222,27 +245,22 @@
         both = pot * (-1.0 / CAP) + motion[at, :]
         out2[at, :] = jnp.where(lane8 < 2 * slots, both, member[at, :])
 
-    def send_block(px):
-        for peer in range(ny):
-
-            @pl.when((px - mx) * (px - mx) + (peer - my) * (peer - my) > 0)
-            def _():
-                pltpu.make_async_remote_copy(
-                    src_ref=out2.at[pl.ds(px * ny + peer, 1)],
-                    dst_ref=got2.at[own],
-                    send_sem=send2,
-                    recv_sem=recv2,
-                    device_id=(px, peer),
-                    device_id_type=MESH,
-                ).start()
-
-    def block_of(step, carry):
-        px = column_of(step)
-        before = column_of((step + nx - 1) % nx)
-        conclude(before)
+    def send_to(px, peer):
+        pltpu.make_async_remote_copy(
+            src_ref=out2.at[pl.ds(px * ny + peer, 1)],
+            dst_ref=got2.at[own],
+            send_sem=send2,
+            recv_sem=recv2,
+            device_id=(px, peer),
+            device_id_type=MESH,
+        ).start()
+
+    def pairs_of(px, between):
         target = points[pl.ds(pl.multiple_of(px * 8, 8), 8), :]
         diagonal = offset8 == px * 8
         for group in range(owned):
+            if group == owned // 2:
+                between()
             base = group * MOST
             there = [
                 [jnp.broadcast_to(rows_ref[f * slots + base + r : f * slots + base + r + 1, :], (8, LANES)) for f in range(4)]
@@ -273,46 +291,44 @@
                 halves[lines, :LANES] = high
                 halves[lines, LANES:] = low
 
-        @pl.when(step > 0)
-        def _():
-            send_block(before)
-
+    def block_of(turn, carry):
+        gone = []
+        for piece in range(3):
+            step = turn * 3 + piece + 1
+            before = column_of(step - 1)
+            conclude(before)
+            pairs_of(column_of(step), lambda: None)
+            gone.append(before)
+            if False:
+                for peer in range(ny):
+                    send_to(before, peer)
+        if not False:
+            for before in gone:
+                for peer in range(ny):
+                    send_to(before, peer)
         return carry
 
-    halves[...] = jnp.zeros_like(halves)
-    lax.fori_loop(0, nx, block_of, 0)
+    pairs_of(column_of(0), lambda: None)
+    lax.fori_loop(0, (nx - 1) // 3, block_of, 0)
     conclude(mx)
-    send_block(mx)
+    for step in range(1, ny):
+        send_to(mx, lax.rem(my + step, ny))
     pltpu.make_async_copy(out2.at[own], got2.at[own], recv2).start()
     pltpu.make_async_copy(out2.at[own], spare2.at[own], send2).start()
+    pick = iota((LANES, owned), 0) == iota((LANES, owned), 1) * MOST
+    stat_rows = jnp.concatenate(stats + [jnp.zeros((LANES - 4, LANES), F32)], axis=0).T
+    for number in range(4):
+        cat_ref[number : number + 1, :] = jnp.sum(
+            jnp.where(pick, stat_rows[:, number : number + 1], 0.0), axis=0, keepdims=True
+        )
+    upper = jnp.where(iota((LANES, LANES), 0) < iota((LANES, LANES), 1), 1.0, 0.0).astype(BF16)
     pltpu.make_async_copy(out2, out2, send2).wait()
     pltpu.make_async_copy(got2, got2, recv2).wait()
-    reply_ref[...] = got2[...]
-
-
-def finish(lab_ref, slot_ref, place_ref, reply_ref, cat_in, index_ref, pot_ref, bind_ref, cat_ref):
-    count = lab_ref.shape[1]
-    groups = slot_ref.shape[1]
-    devices = reply_ref.shape[0]
-    half = groups // LANES
-    owned = groups // devices
-    slots = owned * MOST
-    cat_ref[...] = cat_in[...]
-    label = lab_ref[...]
-    label_high, label_low = label >> 7, label & 127
-    high_hit = iota((half, count), 0) == label_high
-    place = place_ref[...]
-    hot_dest = onehot(place // slots, devices)
-    slot_hit = iota((slots, count), 0) == place % slots
-    slot_row = slot_ref[...]
-    hot_group = onehot(slot_row // owned, devices)
-    upper = jnp.where(iota((LANES, LANES), 0) < iota((LANES, LANES), 1), 1.0, 0.0).astype(BF16)
-
-    answer = reply_ref[...].T
-    pieces = parts_of(answer, 3)
-    kept_of = dot(pieces[0][3 * slots :], hot_group) + dot(pieces[1][3 * slots :], hot_group)
-    group_hit = iota((slots, groups), 0) == (slot_row % owned) * MOST
-    kept_row = jnp.sum(jnp.where(group_hit, kept_of, 0.0), axis=0, keepdims=True)
+    answer = got2[...].T
+    kept_of = pick_lanes(answer[3 * slots : 3 * slots + owned], slot_row // owned)
+    kept_row = jnp.sum(
+        jnp.where(iota((owned, groups), 0) == slot_row % owned, kept_of, 0.0), axis=0, keepdims=True
+    )
     kept8 = jnp.concatenate(
         [kept_row[:, i * LANES : (i + 1) * LANES] for i in range(half)], axis=0
     )
@@ -323,21 +339,24 @@
     for i in range(half - 1):
         running.append(running[-1] + row_total[i : i + 1])
     start8 = start8 + jnp.concatenate(running, axis=0)
-    start_parts = jnp.concatenate(parts_of(start8, 3), axis=0)
-    start_found = dot(start_parts, onehot(label_low, LANES))
-    start_found = start_found[:half] + start_found[half : 2 * half] + start_found[2 * half :]
-    start = jnp.sum(jnp.where(high_hit, start_found, 0.0), axis=0, keepdims=True)
-
-    table = [piece[: 3 * slots] for piece in pieces]
-    values = dot(table[0], hot_dest) + dot(table[1], hot_dest) + dot(table[2], hot_dest)
+    start = jnp.sum(jnp.where(high_hit, pick_lanes(start8, label_low), 0.0), axis=0, keepdims=True)
     chosen = [
-        jnp.sum(jnp.where(slot_hit, values[v * slots : (v + 1) * slots], 0.0), axis=0, keepdims=True)
+        jnp.sum(
+            jnp.where(slot_hit, pick_lanes(answer[v * slots : (v + 1) * slots], dest), 0.0),
+            axis=0, keepdims=True,
+        )
         for v in range(3)
     ]
     kept = chosen[2] >= 0.0
     index_ref[...] = jnp.where(kept, start + chosen[2], -1.0).astype(I32)
     pot_ref[...] = jnp.where(kept, chosen[0], 0.0)
     bind_ref[...] = jnp.where(kept, chosen[1], 0.0)
+
+
+def finish(*refs):
+    half = len(refs) // 2
+    for source, result in zip(refs[:half], refs[half:]):
+        result[...] = source[...]
 
 
 def shards(sizes, positions, velocities, masses, labels, owner_slot, group_cap):
@@ -351,39 +370,39 @@
     wide = lambda width: pltpu.VMEM((devices, width), F32)
     label_row = labels.reshape(1, count)
     slot_row = owner_slot.reshape(1, groups)
-    reply, place, catalog = pl.pallas_call(
+    row = lambda dtype: jax.ShapeDtypeStruct((1, count), dtype)
+    results = (row(I32), row(F32), row(F32), jax.ShapeDtypeStruct((4, owned), F32))
+    inputs = (
+        label_row, labels.reshape(count // LANES, LANES), positions, velocities,
+        masses.reshape(1, count), owner_slot.reshape(groups // LANES, LANES),
+        slot_row, group_cap.reshape(1, groups),
+    )
+    found = pl.pallas_call(
         functools.partial(kernel, sizes),
-        out_shape=(
-            jax.ShapeDtypeStruct((devices, LANES), F32),
-            jax.ShapeDtypeStruct((1, count), I32),
-            jax.ShapeDtypeStruct((4, owned), F32),
-        ),
-        in_specs=[vmem] * 8,
-        out_specs=(vmem,) * 3,
+        out_shape=results,
+        in_specs=[pl.BlockSpec(memory_space=pl.ANY)] * 8,
+        out_specs=(vmem,) * 4,
         scratch_shapes=[
+            *[pltpu.VMEM(array.shape, array.dtype) for array in inputs],
             *[wide(2 * LANES)] * 3,
             *[wide(LANES)] * 3,
             pltpu.VMEM((devices, count), BF16),
             *[wide(LANES)] * 4,
             pltpu.VMEM((slots * 8, 2 * LANES), BF16),
+            pltpu.SemaphoreType.DMA((8,)),
             *[pltpu.SemaphoreType.DMA] * 4,
             pltpu.SemaphoreType.REGULAR,
         ],
         compiler_params=pltpu.CompilerParams(collective_id=0, has_side_effects=True),
         name="unbind",
-    )(
-        label_row, labels.reshape(count // LANES, LANES), positions, velocities,
-        masses.reshape(1, count), owner_slot.reshape(groups // LANES, LANES),
-        slot_row, group_cap.reshape(1, groups),
-    )
-    row = lambda dtype: jax.ShapeDtypeStruct((1, count), dtype)
+    )(*inputs)
     index, pot, bind, catalog = pl.pallas_call(
         finish,
-        out_shape=(row(I32), row(F32), row(F32), jax.ShapeDtypeStruct((4, owned), F32)),
-        in_specs=[vmem] * 5,
+        out_shape=results,
+        in_specs=[vmem] * 4,
         out_specs=(vmem,) * 4,
         name="finish",
-    )(label_row, slot_row, place, reply, catalog)
+    )(*found)
     return (index.reshape(count), pot.reshape(count), bind.reshape(count), catalog)
 
 

time: 33 us -> 30.2 us (0.915)
  Pallas kernels: 32.2 us -> 29.4 us
    pallas_call x2, Pallas kernels: 32.2 us -> 29.4 us  [the longest x1 28 us: shards(): pl.pallas_call(functools.partial(kernel, sizes), out_shape=results, in_sp...]
where the time goes in v3:
time: 30.2 us; the launch traced here: 30 us
  Pallas kernels  29.4 us (97%)
  between operations  0.64 us (2%)
    pallas_call x1, Pallas kernels, shards(): pl.pallas_call(functools.partial(kernel, sizes), out_shape=results, in_sp...  28 us
    pallas_call x1, Pallas kernels, shards(): pl.pallas_call(finish, out_shape=results, in_specs=[vmem] * 4, out_specs=...  1.35 us

profile of v3, /device:TPU:1, one launch (start us, length us, event | category | flops | bytes accessed | tf_op | source)
XLA Modules:
  0.0 30.0 jit_solution(8711439383109596783)
XLA Ops:
  0.6 28.0 %unbind.1 = (s32[1,2048]{1,0:T(1,128)}, f32[1,2048]{1,0:T(1,128)}, f32[1,2048]{1,0:T(1,128)}, f32[4,8]{1,0:T(4,128)}) custom-call(s32[1,2048]{1,0:T(1,128)} %bitcast.9, s32[16,128]{1,0:T(8,128)} %bitcast.10, f32[3,2048]{1,0:T(4,128)} %pos_hbm.1, f32[3,2048]{1,0:T(4,128)} %vel_hbm.1, f32[1,2048]{1,0:T(1,128)} %bitcast.13, s32[8,128]{1,0:T(8,128)} %bitcast.11, ...), custom_call_target="tpu_custom_call" | custom-call | tf_op jit(solution)/shard_map/unbind/pallas_call | solution.py:380
  28.7 1.3 %finish.1 = (s32[1,2048]{1,0:T(1,128)}, f32[1,2048]{1,0:T(1,128)}, f32[1,2048]{1,0:T(1,128)}, f32[4,8]{1,0:T(4,128)}) custom-call(s32[1,2048]{1,0:T(1,128)} %get-tuple-element.12.refs_0_, f32[1,2048]{1,0:T(1,128)} %get-tuple-element.13.refs_1_, f32[1,2048]{1,0:T(1,128)} %get-tuple-element.14.refs_2_, f32[4,8]{1,0:T(4,128)} %get-tuple-element.15.refs_3_), custom_call_target="tpu_custom_call" | custom-call | tf_op jit(solution)/shard_map/finish/pallas_call | solution.py:399

commit v4 on v3

--- a/solution.py
+++ b/solution.py
@@ -113,10 +113,15 @@
     for load in loads:
         load.start()
     barrier = pltpu.get_barrier_semaphore()
-    for step in range(1, nx):
-        pl.semaphore_signal(barrier, inc=1, device_id=(lax.rem(mx + step, nx), my), device_id_type=MESH)
-    for step in range(1, ny):
-        pl.semaphore_signal(barrier, inc=1, device_id=(mx, lax.rem(my + step, ny)), device_id_type=MESH)
+    here = (mx, my)
+
+    def announce(offsets):
+        for dz, dx, dy, dc in offsets:
+            px = ((mx // 4 + dz) % 4) * 4 + (mx + dx) % 4
+            py = ((my // 2 + dy) % 4) * 2 + (my + dc) % 2
+            pl.semaphore_signal(barrier, inc=1, device_id=(px, py), device_id_type=MESH)
+
+    announce(far_first())
     for load in loads:
         load.wait()
 
@@ -177,10 +182,7 @@
     lower = jnp.where(iota((LANES, LANES), 1) < iota((LANES, LANES), 0), 1.0, 0.0).astype(BF16)
     quarter = (iota((1, LANES), 1) % MOST).astype(F32)
 
-    pl.semaphore_wait(barrier, nx + ny - 2)
-    for step in range(1, ny):
-        pl.semaphore_signal(ready, inc=1, device_id=(mx, lax.rem(my + step, ny)), device_id_type=MESH)
-    pl.semaphore_wait(ready, ny - 1)
+    pl.semaphore_wait(barrier, devices - 1)
     here = (mx, my)
     for offset in far_first():
         send_row(here, offset, out1, got1, send1, recv1, ny)
@@ -309,9 +311,15 @@
         return carry
 
     pairs_of(column_of(0), lambda: None)
-    lax.fori_loop(0, (nx - 1) // 3, block_of, 0)
+    lax.fori_loop(0, (nx - 1) // 3 - 1, block_of, 0)
+    for step in range(nx - 3, nx):
+        before = column_of(step - 1)
+        conclude(before)
+        for peer in range(ny):
+            send_to(before, peer)
+        pairs_of(column_of(step), lambda: None)
     conclude(mx)
-    for step in range(1, ny):
+    for step in (4, 5, 2, 3, 6, 7, 1):
         send_to(mx, lax.rem(my + step, ny))
     pltpu.make_async_copy(out2.at[own], got2.at[own], recv2).start()
     pltpu.make_async_copy(out2.at[own], spare2.at[own], send2).start()
@@ -380,7 +388,7 @@
     found = pl.pallas_call(
         functools.partial(kernel, sizes),
         out_shape=results,
-        in_specs=[pl.BlockSpec(memory_space=pl.ANY)] * 8,
+        in_specs=[pl.BlockSpec(memory_space=pltpu.HBM)] * 8,
         out_specs=(vmem,) * 4,
         scratch_shapes=[
             *[pltpu.VMEM(array.shape, array.dtype) for array in inputs],
@@ -393,14 +401,17 @@
             *[pltpu.SemaphoreType.DMA] * 4,
             pltpu.SemaphoreType.REGULAR,
         ],
-        compiler_params=pltpu.CompilerParams(collective_id=0, has_side_effects=True),
+        compiler_params=pltpu.CompilerParams(
+            collective_id=0, has_side_effects=True, vmem_limit_bytes=24 * 2**20
+        ),
         name="unbind",
-    )(*inputs)
+    )(*[pltpu.with_memory_space_constraint(array, pltpu.HBM) for array in inputs])
     index, pot, bind, catalog = pl.pallas_call(
         finish,
         out_shape=results,
         in_specs=[vmem] * 4,
         out_specs=(vmem,) * 4,
+        compiler_params=pltpu.CompilerParams(vmem_limit_bytes=2**20),
         name="finish",
     )(*found)
     return (index.reshape(count), pot.reshape(count), bind.reshape(count), catalog)

time: 30.2 us -> 27.8 us (0.921)
  Pallas kernels: 29.4 us -> 27 us
    pallas_call x1, Pallas kernels: 28 us -> 26.4 us  [shards(): pl.pallas_call(functools.partial(kernel, sizes), out_shape=results, in_sp...]
    pallas_call x1, Pallas kernels: 1.35 us -> 0.61 us  [shards(): pl.pallas_call(finish, out_shape=results, in_specs=[vmem] * 4, out_specs=...]
where the time goes in v4:
time: 27.8 us; the launch traced here: 27.7 us
  Pallas kernels  27 us (97%)
  between operations  0.64 us (2%)
    pallas_call x1, Pallas kernels, shards(): pl.pallas_call(functools.partial(kernel, sizes), out_shape=results, in_sp...  26.4 us
    pallas_call x1, Pallas kernels, shards(): pl.pallas_call(finish, out_shape=results, in_specs=[vmem] * 4, out_specs=...  0.61 us

profile of v4, /device:TPU:1, one launch (start us, length us, event | category | flops | bytes accessed | tf_op | source)
XLA Modules:
  0.0 27.7 jit_solution(17601779097967075434)
XLA Ops:
  0.6 26.4 %unbind.1 = (s32[1,2048]{1,0:T(1,128)S(1)}, f32[1,2048]{1,0:T(1,128)S(1)}, f32[1,2048]{1,0:T(1,128)S(1)}, f32[4,8]{1,0:T(4,128)S(1)}) custom-call(s32[1,2048]{1,0:T(1,128)} %bitcast.9, s32[16,128]{1,0:T(8,128)} %bitcast.10, f32[3,2048]{1,0:T(4,128)} %pos_hbm.1, f32[3,2048]{1,0:T(4,128)} %vel_hbm.1, f32[1,2048]{1,0:T(1,128)} %bitcast.13, s32[8,128]{1,0:T(8,128)} %bitcast.11, ...), custom_call_target="tpu_custom_call" | custom-call | tf_op jit(solution)/shard_map/unbind/pallas_call | solution.py:388
  27.0 0.6 %finish.1 = (s32[1,2048]{1,0:T(1,128)}, f32[1,2048]{1,0:T(1,128)}, f32[1,2048]{1,0:T(1,128)}, f32[4,8]{1,0:T(4,128)}) custom-call(s32[1,2048]{1,0:T(1,128)S(1)} %get-tuple-element.12.refs_0_, f32[1,2048]{1,0:T(1,128)S(1)} %get-tuple-element.13.refs_1_, f32[1,2048]{1,0:T(1,128)S(1)} %get-tuple-element.14.refs_2_, f32[4,8]{1,0:T(4,128)S(1)} %get-tuple-element.15.refs_3_), custom_call_target="tpu_custom_call" | custom-call | tf_op jit(solution)/shard_map/finish/pallas_call | solution.py:409

commit v5 on v4

--- a/solution.py
+++ b/solution.py
@@ -69,28 +69,23 @@
     return offsets[:-1]
 
 
-def send_row(here, offset, out, got, send, recv, ny):
+def near_first():
+    return [(0, 0, 0, 0)] + far_first()[::-1]
+
+
+def peer_at(here, offset):
     mx, my = here
     dz, dx, dy, dc = offset
-    px = ((mx // 4 + dz) % 4) * 4 + (mx + dx) % 4
-    py = ((my // 2 + dy) % 4) * 2 + (my + dc) % 2
-    pltpu.make_async_remote_copy(
-        src_ref=out.at[pl.ds(px * ny + py, 1)],
-        dst_ref=got.at[pl.ds(mx * ny + my, 1)],
-        send_sem=send,
-        recv_sem=recv,
-        device_id=(px, py),
-        device_id_type=MESH,
-    ).start()
+    return (((mx // 4 + dz) % 4) * 4 + (mx + dx) % 4, ((my // 2 + dy) % 4) * 2 + (my + dc) % 2)
 
 
 def kernel(
-    sizes, lab_hbm, lab16_hbm, pos_hbm, vel_hbm, mass_hbm, slot8_hbm, slot_hbm, cap_hbm,
+    sizes, lab_hbm, lab16_hbm, pos_hbm, vel_hbm, mass_hbm, slot8_hbm, slot_hbm, cap_hbm, order_hbm,
     index_ref, pot_ref, bind_ref, cat_ref,
-    lab_ref, lab16_ref, pos_ref, vel_ref, mass_ref, slot8_ref, slot_ref, cap_ref,
+    lab_ref, lab16_ref, pos_ref, vel_ref, mass_ref, slot8_ref, slot_ref, cap_ref, order_ref,
     out1, spare1, got1, out2, spare2, got2, hot_dest,
-    rows_ref, points, motion, member, halves,
-    load_sems, send1, recv1, send2, recv2, ready,
+    rows_ref, motion, member, halves,
+    load_sems, send1, recv1, send2, recv2,
 ):
     nx, ny = sizes
     devices = nx * ny
@@ -107,7 +102,7 @@
         pltpu.make_async_copy(source, place, load_sems.at[number])
         for number, (source, place) in enumerate((
             (lab_hbm, lab_ref), (slot8_hbm, slot8_ref), (lab16_hbm, lab16_ref), (mass_hbm, mass_ref),
-            (pos_hbm, pos_ref), (vel_hbm, vel_ref), (slot_hbm, slot_ref), (cap_hbm, cap_ref),
+            (pos_hbm, pos_ref), (vel_hbm, vel_ref), (slot_hbm, slot_ref), (cap_hbm, cap_ref), (order_hbm, order_ref),
         ))
     ]
     for load in loads:
@@ -115,13 +110,8 @@
     barrier = pltpu.get_barrier_semaphore()
     here = (mx, my)
 
-    def announce(offsets):
-        for dz, dx, dy, dc in offsets:
-            px = ((mx // 4 + dz) % 4) * 4 + (mx + dx) % 4
-            py = ((my // 2 + dy) % 4) * 2 + (my + dc) % 2
-            pl.semaphore_signal(barrier, inc=1, device_id=(px, py), device_id_type=MESH)
-
-    announce(far_first())
+    for offset in far_first():
+        pl.semaphore_signal(barrier, inc=1, device_id=peer_at(here, offset), device_id_type=MESH)
     for load in loads:
         load.wait()
 
@@ -135,24 +125,32 @@
     )
     dest, local_group = owner // owned, owner % owned
 
+    hot_low = onehot(label_low, LANES)
+    high_one = jnp.where(high_hit, 1.0, 0.0)
+    none = jnp.zeros((half, LANES), F32)
+    prior = jnp.concatenate([
+        jnp.concatenate([
+            high_one[:, other * LANES : (other + 1) * LANES] if other < block else none
+            for other in range(blocks)
+        ], axis=1)
+        for block in range(blocks)
+    ], axis=0).astype(BF16)
+    tables = dot_nt(prior, hot_low)
     columns = jnp.concatenate(
         [lab16_ref[...], jnp.zeros((LANES - blocks, LANES), I32)], axis=0
     ).astype(F32).T.astype(I32)
+    triangle = jnp.where(iota((LANES, LANES), 0) < iota((LANES, LANES), 1), 1.0, 0.0)
     ranks = []
-    triangle = iota((LANES, LANES), 0) < iota((LANES, LANES), 1)
     for block in range(blocks):
-        mine = label[:, block * LANES : (block + 1) * LANES]
-        ranks.append(jnp.zeros((8, LANES), I32))
-    for other in range(blocks):
-        column = jnp.broadcast_to(columns[:, other : other + 1], (LANES, LANES))
-        for block in range(other, blocks):
-            mine = label[:, block * LANES : (block + 1) * LANES]
-            same = column == mine
-            if block == other:
-                same = same & triangle
-            hits = jnp.where(same, 1, 0)
-            ranks[block] = ranks[block] + jnp.sum(hits.reshape(LANES // 8, 8, LANES), axis=0)
-    rank = jnp.concatenate([jnp.sum(r, axis=0, keepdims=True) for r in ranks], axis=1)
+        lanes = slice(block * LANES, (block + 1) * LANES)
+        column = jnp.broadcast_to(columns[:, block : block + 1], (LANES, LANES))
+        within = jnp.where(column == label[:, lanes], triangle, 0.0)
+        before = jnp.where(
+            high_hit[:, lanes], pick_lanes(tables[block * half : (block + 1) * half], label_low[:, lanes]), 0.0
+        )
+        within = jnp.sum(within.reshape(LANES // half, half, LANES), axis=0)
+        ranks.append(jnp.sum(before + within, axis=0, keepdims=True))
+    rank = jnp.concatenate(ranks, axis=1).astype(I32)
     slot = local_group * MOST + rank
 
     hot_dest[...] = onehot(dest, devices)
@@ -179,28 +177,56 @@
     limit_parts = jnp.concatenate([limits // 64, limits % 64], axis=0).astype(F32).astype(BF16)
     limit = dot_nt(limit_parts, mine)
     limit = limit[0:1] * 64.0 + limit[1:2]
-    lower = jnp.where(iota((LANES, LANES), 1) < iota((LANES, LANES), 0), 1.0, 0.0).astype(BF16)
+    away = order_ref[...]
+    source = (((mx // 4 + away[0:1]) & 3) * 4 + ((mx + away[1:2]) & 3)) * ny + (
+        ((my // 2 + away[2:3]) & 3) * 2 + ((my + away[3:4]) & 1)
+    )
+    source = jnp.broadcast_to(source.astype(F32), (LANES, LANES))
+    lower = jnp.where(source < source.T, 1.0, 0.0).astype(BF16)
     quarter = (iota((1, LANES), 1) % MOST).astype(F32)
 
     pl.semaphore_wait(barrier, devices - 1)
     here = (mx, my)
+    places = near_first()
     for offset in far_first():
-        send_row(here, offset, out1, got1, send1, recv1, ny)
+        back = places.index(tuple((size - step) % size for step, size in zip(offset, (4, 4, 4, 2))))
+        px, py = peer_at(here, offset)
+        pltpu.make_async_remote_copy(
+            src_ref=out1.at[pl.ds(px * ny + py, 1)],
+            dst_ref=got1.at[pl.ds(back, 1)],
+            send_sem=send1,
+            recv_sem=recv1,
+            device_id=(px, py),
+            device_id_type=MESH,
+        ).start()
     own = pl.ds(me, 1)
-    pltpu.make_async_copy(out1.at[own], got1.at[own], recv1).start()
+    pltpu.make_async_copy(out1.at[own], got1.at[pl.ds(0, 1)], recv1).start()
     pltpu.make_async_copy(out1.at[own], spare1.at[own], send1).start()
+
+    lane = iota((1, LANES), 1)
+    lane8 = iota((8, LANES), 1)
+    offset8 = lane8 - iota((8, LANES), 0)
+
+    def row_of(ref, at):
+        return jnp.broadcast_to(ref[at : at + 1, :], (8, LANES))
+
+    def column_of(block, at):
+        return jnp.broadcast_to(block[:, at : at + 1], (8, LANES))
+
+    def inverse_of(target, there):
+        ax, ay, az = [t - h for t, h in zip(target, there)]
+        return lax.rsqrt(ax * ax + ay * ay + az * az + SOFTENING_SQ)
+
+    pltpu.make_async_copy(got1, got1, recv1).wait()
     pltpu.make_async_copy(out1, out1, send1).wait()
-    pltpu.make_async_copy(got1, got1, recv1).wait()
 
     first = got1[:, :LANES]
-    lane = iota((1, LANES), 1)
     is_mass = lane < slots
     valid = is_mass & (first > 0.0)
     tally = quad_sum(jnp.where(valid, 1.0, 0.0))
     member_rank = dot(lower, tally.astype(BF16)) + quarter
     keep = valid & (member_rank < limit)
-    points[...] = jnp.where(is_mass & ~keep, 0.0, first)
-    rows_ref[...] = points[...].T
+    rows_ref[...] = jnp.where(is_mass & ~keep, 0.0, first).T
     kept_mass = jnp.where(keep, first, 0.0)
     kept_total = quad_sum(jnp.sum(jnp.where(keep, 1.0, 0.0), axis=0, keepdims=True))
     mass_sum = quad_sum(jnp.sum(kept_mass, axis=0, keepdims=True))
@@ -225,21 +251,11 @@
             (devices, LANES),
         ),
     )
-    offset8 = iota((8, LANES), 1) - iota((8, LANES), 0)
-    lane8 = iota((8, LANES), 1)
     spot8 = lane8 % slots
     ones = jnp.ones((2 * LANES, LANES), BF16)
 
-    def order(digit):
-        half, odd = digit // 2, digit % 2
-        return (1 - half) * (2 - odd) + half * (3 - 3 * odd)
-
-    def column_of(step):
-        dz, dx = order(step // 4), order(step % 4)
-        return ((mx // 4 + dz) % 4) * 4 + (mx + dx) % 4
-
-    def conclude(px):
-        at = pl.ds(pl.multiple_of(px * 8, 8), 8)
+    def conclude(block):
+        at = pl.ds(block * 8, 8)
         sums = dot(halves[...], ones)
         pot = jnp.zeros((8, LANES), F32)
         for spot in range(slots):
@@ -247,82 +263,52 @@
         both = pot * (-1.0 / CAP) + motion[at, :]
         out2[at, :] = jnp.where(lane8 < 2 * slots, both, member[at, :])
 
-    def send_to(px, peer):
-        pltpu.make_async_remote_copy(
-            src_ref=out2.at[pl.ds(px * ny + peer, 1)],
-            dst_ref=got2.at[own],
-            send_sem=send2,
-            recv_sem=recv2,
-            device_id=(px, peer),
-            device_id_type=MESH,
-        ).start()
-
-    def pairs_of(px, between):
-        target = points[pl.ds(pl.multiple_of(px * 8, 8), 8), :]
-        diagonal = offset8 == px * 8
+    def pairs_of(block):
+        targets = got1[block * 8 : block * 8 + 8, :LANES]
+        itself = offset8 == block * 8
         for group in range(owned):
-            if group == owned // 2:
-                between()
             base = group * MOST
-            there = [
-                [jnp.broadcast_to(rows_ref[f * slots + base + r : f * slots + base + r + 1, :], (8, LANES)) for f in range(4)]
-                for r in range(MOST)
-            ]
+            there = [[row_of(rows_ref, f * slots + base + r) for f in range(4)] for r in range(MOST)]
             totals = []
             for r in range(MOST):
-                spot = base + r
-                px_, py_, pz_ = [
-                    jnp.broadcast_to(target[:, f * slots + spot : f * slots + spot + 1], (8, LANES))
-                    for f in range(1, 4)
-                ]
+                target = [column_of(targets, f * slots + base + r) for f in range(1, 4)]
                 total = None
                 for other in range(MOST):
-                    ax = px_ - there[other][1]
-                    ay = py_ - there[other][2]
-                    az = pz_ - there[other][3]
-                    inverse = lax.rsqrt(ax * ax + ay * ay + az * az + SOFTENING_SQ)
+                    value = inverse_of(target, there[other][1:])
                     if r == other:
-                        inverse = jnp.where(diagonal, 0.0, inverse)
-                    term = inverse * there[other][0]
+                        value = jnp.where(itself, 0.0, value)
+                    term = value * there[other][0]
                     total = term if total is None else total + term
                 totals.append(total)
             for pair in range(0, MOST, 2):
-                two = jnp.concatenate(totals[pair : pair + 2], axis=0)
-                high, low = parts_of(two, 2)
-                lines = pl.ds((base + pair) * 8, 16)
+                high, low = parts_of(jnp.concatenate(totals[pair : pair + 2], axis=0), 2)
+                lines = pl.ds((group * MOST + pair) * 8, 16)
                 halves[lines, :LANES] = high
                 halves[lines, LANES:] = low
 
-    def block_of(turn, carry):
-        gone = []
-        for piece in range(3):
-            step = turn * 3 + piece + 1
-            before = column_of(step - 1)
-            conclude(before)
-            pairs_of(column_of(step), lambda: None)
-            gone.append(before)
-            if False:
-                for peer in range(ny):
-                    send_to(before, peer)
-        if not False:
-            for before in gone:
-                for peer in range(ny):
-                    send_to(before, peer)
-        return carry
-
-    pairs_of(column_of(0), lambda: None)
-    lax.fori_loop(0, (nx - 1) // 3 - 1, block_of, 0)
-    for step in range(nx - 3, nx):
-        before = column_of(step - 1)
-        conclude(before)
-        for peer in range(ny):
-            send_to(before, peer)
-        pairs_of(column_of(step), lambda: None)
-    conclude(mx)
-    for step in (4, 5, 2, 3, 6, 7, 1):
-        send_to(mx, lax.rem(my + step, ny))
-    pltpu.make_async_copy(out2.at[own], got2.at[own], recv2).start()
-    pltpu.make_async_copy(out2.at[own], spare2.at[own], send2).start()
+    def send_block(block):
+        for place in range(block * 8 + 7, block * 8 - 1, -1):
+            if place:
+                pltpu.make_async_remote_copy(
+                    src_ref=out2.at[pl.ds(place, 1)],
+                    dst_ref=got2.at[own],
+                    send_sem=send2,
+                    recv_sem=recv2,
+                    device_id=peer_at(here, places[place]),
+                    device_id_type=MESH,
+                ).start()
+
+    last = devices // 8 - 1
+    for block in range(last, -1, -1):
+        if block < last:
+            conclude(block + 1)
+        pairs_of(block)
+        if block < last:
+            send_block(block + 1)
+    conclude(0)
+    send_block(0)
+    pltpu.make_async_copy(out2.at[pl.ds(0, 1)], got2.at[own], recv2).start()
+    pltpu.make_async_copy(out2.at[pl.ds(0, 1)], spare2.at[own], send2).start()
     pick = iota((LANES, owned), 0) == iota((LANES, owned), 1) * MOST
     stat_rows = jnp.concatenate(stats + [jnp.zeros((LANES - 4, LANES), F32)], axis=0).T
     for number in range(4):
@@ -384,22 +370,23 @@
         label_row, labels.reshape(count // LANES, LANES), positions, velocities,
         masses.reshape(1, count), owner_slot.reshape(groups // LANES, LANES),
         slot_row, group_cap.reshape(1, groups),
+        jnp.array(near_first(), I32).T,
     )
     found = pl.pallas_call(
         functools.partial(kernel, sizes),
         out_shape=results,
-        in_specs=[pl.BlockSpec(memory_space=pltpu.HBM)] * 8,
+        in_specs=[pl.BlockSpec(memory_space=pltpu.HBM)] * 9,
         out_specs=(vmem,) * 4,
         scratch_shapes=[
             *[pltpu.VMEM(array.shape, array.dtype) for array in inputs],
             *[wide(2 * LANES)] * 3,
             *[wide(LANES)] * 3,
             pltpu.VMEM((devices, count), BF16),
-            *[wide(LANES)] * 4,
+            wide(LANES),
+            *[wide(LANES)] * 2,
             pltpu.VMEM((slots * 8, 2 * LANES), BF16),
-            pltpu.SemaphoreType.DMA((8,)),
+            pltpu.SemaphoreType.DMA((9,)),
             *[pltpu.SemaphoreType.DMA] * 4,
-            pltpu.SemaphoreType.REGULAR,
         ],
         compiler_params=pltpu.CompilerParams(
             collective_id=0, has_side_effects=True, vmem_limit_bytes=24 * 2**20

time: 27.8 us -> 26.2 us (0.942)
  Pallas kernels: 27 us -> 25.4 us
    pallas_call x1, Pallas kernels: 26.4 us -> 24.8 us  [shards(): pl.pallas_call(functools.partial(kernel, sizes), out_shape=results, in_sp...]
where the time goes in v5:
time: 26.2 us; the launch traced here: 26.1 us
  Pallas kernels  25.4 us (97%)
  between operations  0.64 us (2%)
    pallas_call x1, Pallas kernels, shards(): pl.pallas_call(functools.partial(kernel, sizes), out_shape=results, in_sp...  24.8 us
    pallas_call x1, Pallas kernels, shards(): pl.pallas_call(finish, out_shape=results, in_specs=[vmem] * 4, out_specs=...  0.61 us

profile of v5, /device:TPU:1, one launch (start us, length us, event | category | flops | bytes accessed | tf_op | source)
XLA Modules:
  0.0 26.1 jit_solution(4014162923754939044)
XLA Ops:
  0.6 24.8 %unbind.1 = (s32[1,2048]{1,0:T(1,128)S(1)}, f32[1,2048]{1,0:T(1,128)S(1)}, f32[1,2048]{1,0:T(1,128)S(1)}, f32[4,8]{1,0:T(4,128)S(1)}) custom-call(s32[1,2048]{1,0:T(1,128)} %bitcast.9, s32[16,128]{1,0:T(8,128)} %bitcast.10, f32[3,2048]{1,0:T(4,128)} %pos_hbm.1, f32[3,2048]{1,0:T(4,128)} %vel_hbm.1, f32[1,2048]{1,0:T(1,128)} %bitcast.13, s32[8,128]{1,0:T(8,128)} %bitcast.11, ...), custom_call_target="tpu_custom_call" | custom-call | tf_op jit(solution)/shard_map/unbind/pallas_call | solution.py:375
  25.5 0.6 %finish.1 = (s32[1,2048]{1,0:T(1,128)}, f32[1,2048]{1,0:T(1,128)}, f32[1,2048]{1,0:T(1,128)}, f32[4,8]{1,0:T(4,128)}) custom-call(s32[1,2048]{1,0:T(1,128)S(1)} %get-tuple-element.12.refs_0_, f32[1,2048]{1,0:T(1,128)S(1)} %get-tuple-element.13.refs_1_, f32[1,2048]{1,0:T(1,128)S(1)} %get-tuple-element.14.refs_2_, f32[4,8]{1,0:T(4,128)S(1)} %get-tuple-element.15.refs_3_), custom_call_target="tpu_custom_call" | custom-call | tf_op jit(solution)/shard_map/finish/pallas_call | solution.py:396

commit v6 on v5

--- a/solution.py
+++ b/solution.py
@@ -105,12 +105,13 @@
             (pos_hbm, pos_ref), (vel_hbm, vel_ref), (slot_hbm, slot_ref), (cap_hbm, cap_ref), (order_hbm, order_ref),
         ))
     ]
-    for load in loads:
-        load.start()
     barrier = pltpu.get_barrier_semaphore()
     here = (mx, my)
 
-    for offset in far_first():
+    for number, offset in enumerate(far_first()):
+        if number == 14:
+            for load in loads:
+                load.start()
         pl.semaphore_signal(barrier, inc=1, device_id=peer_at(here, offset), device_id_type=MESH)
     for load in loads:
         load.wait()
@@ -158,18 +159,13 @@
     fields = [mass_ref[...], pos_ref[0:1, :], pos_ref[1:2, :], pos_ref[2:3, :],
               vel_ref[0:1, :], vel_ref[1:2, :], vel_ref[2:3, :]]
     split = [[part.astype(F32) for part in parts_of(field, 3)] for field in fields]
-    for half_row in range(2):
-        rows = None
-        for part in range(3):
-            chosen = [
-                jnp.where(slot_hit, split[f][part], 0.0).astype(BF16)
-                for f in range(half_row * 4, min(half_row * 4 + 4, 7))
-            ]
-            if half_row == 1:
-                chosen.append(jnp.zeros((slots, count), BF16))
-            product = dot_nt(hot_dest[...], jnp.concatenate(chosen, axis=0))
-            rows = product if rows is None else rows + product
-        out1[:, half_row * LANES : (half_row + 1) * LANES] = rows
+    outgoing = None
+    for part in range(3):
+        chosen = [jnp.where(slot_hit, split[f][part], 0.0).astype(BF16) for f in range(7)]
+        chosen.append(jnp.zeros((slots, count), BF16))
+        product = dot_nt(hot_dest[...], jnp.concatenate(chosen, axis=0))
+        outgoing = product if outgoing is None else outgoing + product
+    out1[...] = outgoing
 
     slot_row = slot_ref[...]
     mine = jnp.where(iota((LANES, groups), 0) // MOST == slot_row - me * owned, 1.0, 0.0).astype(BF16)
@@ -183,6 +179,9 @@
     )
     source = jnp.broadcast_to(source.astype(F32), (LANES, LANES))
     lower = jnp.where(source < source.T, 1.0, 0.0).astype(BF16)
+    quad = jnp.where(
+        iota((LANES, LANES), 0) // MOST == iota((LANES, LANES), 1) // MOST, 1.0, 0.0
+    ).astype(BF16)
     quarter = (iota((1, LANES), 1) % MOST).astype(F32)
 
     pl.semaphore_wait(barrier, devices - 1)
@@ -223,11 +222,12 @@
     first = got1[:, :LANES]
     is_mass = lane < slots
     valid = is_mass & (first > 0.0)
-    tally = quad_sum(jnp.where(valid, 1.0, 0.0))
-    member_rank = dot(lower, tally.astype(BF16)) + quarter
+    earlier = dot(lower, jnp.where(valid, 1.0, 0.0).astype(BF16))
+    member_rank = dot(earlier.astype(BF16), quad) + quarter
     keep = valid & (member_rank < limit)
-    rows_ref[...] = jnp.where(is_mass & ~keep, 0.0, first).T
     kept_mass = jnp.where(keep, first, 0.0)
+    rows_ref[slots:] = first.T[slots:]
+    rows_ref[:slots] = kept_mass.T[:slots]
     kept_total = quad_sum(jnp.sum(jnp.where(keep, 1.0, 0.0), axis=0, keepdims=True))
     mass_sum = quad_sum(jnp.sum(kept_mass, axis=0, keepdims=True))
     second = got1[:, LANES:]
@@ -239,7 +239,7 @@
         stats.append(bulk)
         apart = (speed - bulk) * (speed - bulk)
         energy = apart if energy is None else energy + apart
-    motion[...] = jnp.where((lane >= slots) & (lane < 2 * slots), pltpu.roll(0.5 * energy, slots, 1), 0.0)
+    motion[...] = jnp.where(lane < slots, 0.5 * energy, 0.0)
     rank_or_not = jnp.where(keep, member_rank, -1.0)
     member[...] = jnp.where(
         lane < 3 * slots,
@@ -299,12 +299,19 @@
                 ).start()
 
     last = devices // 8 - 1
+    gone = []
     for block in range(last, -1, -1):
-        if block < last:
+        if block < last - 1:
             conclude(block + 1)
+            gone.append(block + 1)
         pairs_of(block)
-        if block < last:
-            send_block(block + 1)
+        if block == last:
+            conclude(block)
+            gone.append(block)
+        if block >= last - 2 or block <= 5 or block % 2 == 0:
+            for ready in gone:
+                send_block(ready)
+            gone = []
     conclude(0)
     send_block(0)
     pltpu.make_async_copy(out2.at[pl.ds(0, 1)], got2.at[own], recv2).start()
@@ -328,11 +335,12 @@
     )
     kept_parts = parts_of(kept8, 2)
     start8 = dot(kept_parts[0], upper) + dot(kept_parts[1], upper)
-    row_total = jnp.sum(kept8, axis=1, keepdims=True)
-    running = [jnp.zeros((1, 1), F32)]
-    for i in range(half - 1):
-        running.append(running[-1] + row_total[i : i + 1])
-    start8 = start8 + jnp.concatenate(running, axis=0)
+    ahead = jnp.broadcast_to(jnp.sum(kept8, axis=1, keepdims=True), (half, LANES))
+    row8 = iota((half, LANES), 0)
+    ahead = jnp.where(row8 >= 1, pltpu.roll(ahead, 1, 0), 0.0)
+    for step in (1, 2, 4):
+        ahead = ahead + jnp.where(row8 >= step, pltpu.roll(ahead, step, 0), 0.0)
+    start8 = start8 + ahead
     start = jnp.sum(jnp.where(high_hit, pick_lanes(start8, label_low), 0.0), axis=0, keepdims=True)
     chosen = [
         jnp.sum(
@@ -343,8 +351,8 @@
     ]
     kept = chosen[2] >= 0.0
     index_ref[...] = jnp.where(kept, start + chosen[2], -1.0).astype(I32)
-    pot_ref[...] = jnp.where(kept, chosen[0], 0.0)
-    bind_ref[...] = jnp.where(kept, chosen[1], 0.0)
+    pot_ref[...] = jnp.where(kept, chosen[1], 0.0)
+    bind_ref[...] = jnp.where(kept, chosen[0], 0.0)
 
 
 def finish(*refs):

time: 26.2 us -> 26.1 us (level)
  no operation moved by 1% of the time
where the time goes in v6:
time: 26.1 us; the launch traced here: 26 us
  Pallas kernels  25.4 us (97%)
  between operations  0.64 us (2%)
    pallas_call x1, Pallas kernels, shards(): pl.pallas_call(functools.partial(kernel, sizes), out_shape=results, in_sp...  24.7 us
    pallas_call x1, Pallas kernels, shards(): pl.pallas_call(finish, out_shape=results, in_specs=[vmem] * 4, out_specs=...  0.61 us

profile of v6, /device:TPU:1, one launch (start us, length us, event | category | flops | bytes accessed | tf_op | source)
XLA Modules:
  0.0 26.0 jit_solution(4919713173830884237)
XLA Ops:
  0.6 24.7 %unbind.1 = (s32[1,2048]{1,0:T(1,128)S(1)}, f32[1,2048]{1,0:T(1,128)S(1)}, f32[1,2048]{1,0:T(1,128)S(1)}, f32[4,8]{1,0:T(4,128)S(1)}) custom-call(s32[1,2048]{1,0:T(1,128)} %bitcast.9, s32[16,128]{1,0:T(8,128)} %bitcast.10, f32[3,2048]{1,0:T(4,128)} %pos_hbm.1, f32[3,2048]{1,0:T(4,128)} %vel_hbm.1, f32[1,2048]{1,0:T(1,128)} %bitcast.13, s32[8,128]{1,0:T(8,128)} %bitcast.11, ...), custom_call_target="tpu_custom_call" | custom-call | tf_op jit(solution)/shard_map/unbind/pallas_call | solution.py:383
  25.4 0.6 %finish.1 = (s32[1,2048]{1,0:T(1,128)}, f32[1,2048]{1,0:T(1,128)}, f32[1,2048]{1,0:T(1,128)}, f32[4,8]{1,0:T(4,128)}) custom-call(s32[1,2048]{1,0:T(1,128)S(1)} %get-tuple-element.12.refs_0_, f32[1,2048]{1,0:T(1,128)S(1)} %get-tuple-element.13.refs_1_, f32[1,2048]{1,0:T(1,128)S(1)} %get-tuple-element.14.refs_2_, f32[4,8]{1,0:T(4,128)S(1)} %get-tuple-element.15.refs_3_), custom_call_target="tpu_custom_call" | custom-call | tf_op jit(solution)/shard_map/finish/pallas_call | solution.py:404

commit v7 on v6

--- a/solution.py
+++ b/solution.py
@@ -217,7 +217,6 @@
         return lax.rsqrt(ax * ax + ay * ay + az * az + SOFTENING_SQ)
 
     pltpu.make_async_copy(got1, got1, recv1).wait()
-    pltpu.make_async_copy(out1, out1, send1).wait()
 
     first = got1[:, :LANES]
     is_mass = lane < slots
@@ -323,7 +322,6 @@
             jnp.where(pick, stat_rows[:, number : number + 1], 0.0), axis=0, keepdims=True
         )
     upper = jnp.where(iota((LANES, LANES), 0) < iota((LANES, LANES), 1), 1.0, 0.0).astype(BF16)
-    pltpu.make_async_copy(out2, out2, send2).wait()
     pltpu.make_async_copy(got2, got2, recv2).wait()
     answer = got2[...].T
     kept_of = pick_lanes(answer[3 * slots : 3 * slots + owned], slot_row // owned)
@@ -353,12 +351,21 @@
     index_ref[...] = jnp.where(kept, start + chosen[2], -1.0).astype(I32)
     pot_ref[...] = jnp.where(kept, chosen[1], 0.0)
     bind_ref[...] = jnp.where(kept, chosen[0], 0.0)
+    pltpu.make_async_copy(out1, out1, send1).wait()
+    pltpu.make_async_copy(out2, out2, send2).wait()
 
 
 def finish(*refs):
-    half = len(refs) // 2
-    for source, result in zip(refs[:half], refs[half:]):
-        result[...] = source[...]
+    sems = refs[-1]
+    half = (len(refs) - 1) // 2
+    copies = [
+        pltpu.make_async_copy(source, result, sems.at[number])
+        for number, (source, result) in enumerate(zip(refs[:half], refs[half:-1]))
+    ]
+    for copy in copies:
+        copy.start()
+    for copy in copies:
+        copy.wait()
 
 
 def shards(sizes, positions, velocities, masses, labels, owner_slot, group_cap):
@@ -405,7 +412,8 @@
         finish,
         out_shape=results,
         in_specs=[vmem] * 4,
-        out_specs=(vmem,) * 4,
+        out_specs=(pl.BlockSpec(memory_space=pltpu.HBM),) * 4,
+        scratch_shapes=[pltpu.SemaphoreType.DMA((4,))],
         compiler_params=pltpu.CompilerParams(vmem_limit_bytes=2**20),
         name="finish",
     )(*found)

time: 26.1 us -> 26.1 us (level)
  no operation moved by 1% of the time
where the time goes in v7:
time: 26.1 us; the launch traced here: 26 us
  Pallas kernels  25.4 us (97%)
  between operations  0.64 us (2%)
    pallas_call x1, Pallas kernels, shards(): pl.pallas_call(functools.partial(kernel, sizes), out_shape=results, in_sp...  24.8 us
    pallas_call x1, Pallas kernels, shards(): pl.pallas_call(finish, out_shape=results, in_specs=[vmem] * 4, out_specs=...  0.65 us

profile of v7, /device:TPU:1, one launch (start us, length us, event | category | flops | bytes accessed | tf_op | source)
XLA Modules:
  0.0 26.0 jit_solution(7183612291359218206)
XLA Ops:
  0.6 24.8 %unbind.1 = (s32[1,2048]{1,0:T(1,128)S(1)}, f32[1,2048]{1,0:T(1,128)S(1)}, f32[1,2048]{1,0:T(1,128)S(1)}, f32[4,8]{1,0:T(4,128)S(1)}) custom-call(s32[1,2048]{1,0:T(1,128)} %bitcast.9, s32[16,128]{1,0:T(8,128)} %bitcast.10, f32[3,2048]{1,0:T(4,128)} %pos_hbm.1, f32[3,2048]{1,0:T(4,128)} %vel_hbm.1, f32[1,2048]{1,0:T(1,128)} %bitcast.13, s32[8,128]{1,0:T(8,128)} %bitcast.11, ...), custom_call_target="tpu_custom_call" | custom-call | tf_op jit(solution)/shard_map/unbind/pallas_call | solution.py:390
  25.4 0.6 %finish.1 = (s32[1,2048]{1,0:T(1,128)}, f32[1,2048]{1,0:T(1,128)}, f32[1,2048]{1,0:T(1,128)}, f32[4,8]{1,0:T(4,128)}) custom-call(s32[1,2048]{1,0:T(1,128)S(1)} %get-tuple-element.12.refs_0_, f32[1,2048]{1,0:T(1,128)S(1)} %get-tuple-element.13.refs_1_, f32[1,2048]{1,0:T(1,128)S(1)} %get-tuple-element.14.refs_2_, f32[4,8]{1,0:T(4,128)S(1)} %get-tuple-element.15.refs_3_), custom_call_target="tpu_custom_call" | custom-call | tf_op jit(solution)/shard_map/finish/pallas_call | solution.py:411

commit v8 on v6

--- a/solution.py
+++ b/solution.py
@@ -342,12 +342,11 @@
         ahead = ahead + jnp.where(row8 >= step, pltpu.roll(ahead, step, 0), 0.0)
     start8 = start8 + ahead
     start = jnp.sum(jnp.where(high_hit, pick_lanes(start8, label_low), 0.0), axis=0, keepdims=True)
+    first_pieces = [dot(piece, hot_dest[...]) for piece in parts_of(answer[:slots], 3)]
+    found = [first_pieces[0] + first_pieces[1] + first_pieces[2]]
+    found += [pick_lanes(answer[v * slots : (v + 1) * slots], dest) for v in (1, 2)]
     chosen = [
-        jnp.sum(
-            jnp.where(slot_hit, pick_lanes(answer[v * slots : (v + 1) * slots], dest), 0.0),
-            axis=0, keepdims=True,
-        )
-        for v in range(3)
+        jnp.sum(jnp.where(slot_hit, value, 0.0), axis=0, keepdims=True) for value in found
     ]
     kept = chosen[2] >= 0.0
     index_ref[...] = jnp.where(kept, start + chosen[2], -1.0).astype(I32)

time: 26.1 us -> 26.1 us (level)
  no operation moved by 1% of the time
where the time goes in v8:
time: 26.1 us; the launch traced here: 26 us
  Pallas kernels  25.3 us (97%)
  between operations  0.64 us (2%)
    pallas_call x1, Pallas kernels, shards(): pl.pallas_call(functools.partial(kernel, sizes), out_shape=results, in_sp...  24.7 us
    pallas_call x1, Pallas kernels, shards(): pl.pallas_call(finish, out_shape=results, in_specs=[vmem] * 4, out_specs=...  0.61 us

profile of v8, /device:TPU:1, one launch (start us, length us, event | category | flops | bytes accessed | tf_op | source)
XLA Modules:
  0.0 26.0 jit_solution(9741688881024122218)
XLA Ops:
  0.6 24.7 %unbind.1 = (s32[1,2048]{1,0:T(1,128)S(1)}, f32[1,2048]{1,0:T(1,128)S(1)}, f32[1,2048]{1,0:T(1,128)S(1)}, f32[4,8]{1,0:T(4,128)S(1)}) custom-call(s32[1,2048]{1,0:T(1,128)} %bitcast.9, s32[16,128]{1,0:T(8,128)} %bitcast.10, f32[3,2048]{1,0:T(4,128)} %pos_hbm.1, f32[3,2048]{1,0:T(4,128)} %vel_hbm.1, f32[1,2048]{1,0:T(1,128)} %bitcast.13, s32[8,128]{1,0:T(8,128)} %bitcast.11, ...), custom_call_target="tpu_custom_call" | custom-call | tf_op jit(solution)/shard_map/unbind/pallas_call | solution.py:382
  25.3 0.6 %finish.1 = (s32[1,2048]{1,0:T(1,128)}, f32[1,2048]{1,0:T(1,128)}, f32[1,2048]{1,0:T(1,128)}, f32[4,8]{1,0:T(4,128)}) custom-call(s32[1,2048]{1,0:T(1,128)S(1)} %get-tuple-element.12.refs_0_, f32[1,2048]{1,0:T(1,128)S(1)} %get-tuple-element.13.refs_1_, f32[1,2048]{1,0:T(1,128)S(1)} %get-tuple-element.14.refs_2_, f32[4,8]{1,0:T(4,128)S(1)} %get-tuple-element.15.refs_3_), custom_call_target="tpu_custom_call" | custom-call | tf_op jit(solution)/shard_map/finish/pallas_call | solution.py:403
